TPU v7x, 512 devices: a whole 4x4x16 slice. The times are simulated.
512 devices in a mesh: rows: 64 (over y, z), cols: 8 (over x, core).
Axes of the slice: x: 4, y: 4, z: 16, core: 2. Of those that a mesh axis runs over, the one named last changes fastest.
Arguments:
- images: float32 [512, 32, 128], P('rows'), may hold values from -6 to 6
- gauge_pixel: int32 [131072], P('rows'), may hold values from 0 to 32767
- row_mask: int32 [131072], P('rows'), may hold values 0 or 1
- gauge_counts: int32 [64], P('rows'), may hold values from 1 to 2048, as said below
- targets: float32 [131072], P('rows'), may hold values from -10 to 10
- theta: float32 [64, 8], replicated, may hold values from -2.5 to 2.5
- amplitude: float32 [64], replicated, may hold values from 0.5 to 1.5
- damping: float32 [], replicated, may hold values from 0.05 to 0.3
Outputs:
- r_factor: float32 [512, 512], replicated
- new_theta: float32 [64, 8], replicated
- predicted: float32 [131072], P(('rows', 'cols'))
Inputs may be any that keep to these rules, and one draw needn't show every extreme that they name: The slots in use on an index of rows are its first gauge_counts slots; one index of rows uses all 2048.
All inputs are finite; a program needn't handle non-finite values. No bound on the sum of `row_mask` on one device may be relied on, other than what follows from the above.
Results may differ from a plain program's by a relative error of at most 0.0003.
Values sent between devices are 32-bit elements; how exact they have to be, the bound alone decides.
A program may use at most 64 MiB of HBM per device.

v0:
```python
import jax
import jax.numpy as jnp
from jax import lax
from jax.sharding import PartitionSpec as P

BLOCK = 256


y_orders = [0, 1, 0, 2, 1, 0, 0, 0]
x_orders = [0, 0, 1, 0, 1, 2, 0, 2]
sigmas = [1.5, 1.5, 1.5, 1.5, 1.5, 1.5, 3.0, 3.0]


def kernel_values(spacing, deriv_order, width_sigma):
    envelope = jnp.exp(-spacing * spacing / (2.0 * width_sigma * width_sigma))
    if deriv_order == 1:
        return -spacing / width_sigma**2 * envelope
    if deriv_order == 2:
        return (spacing * spacing / width_sigma**4 - 1.0 / width_sigma**2) * envelope
    return envelope


def kernel_table(length, deriv_order, width_sigma):
    places = jnp.arange(length)
    spacing = (places[:, None] - places[None, :]).astype(jnp.float32)
    sample = jnp.arange(-12, 13).astype(jnp.float32)
    scaling = jnp.sqrt(jnp.sum(kernel_values(sample, deriv_order, width_sigma) ** 2))
    return kernel_values(spacing, deriv_order, width_sigma) / scaling


def features(clip_tiles):
    height = clip_tiles.shape[1]
    breadth = clip_tiles.shape[2]
    left_tabs = jnp.stack(
        [kernel_table(height, y_orders[which], sigmas[which]) for which in range(8)]
    )
    right_tabs = jnp.stack(
        [kernel_table(breadth, x_orders[which], sigmas[which]) for which in range(8)]
    )
    partial_conv = jnp.einsum(
        "kij,cjw->kciw", left_tabs, clip_tiles, precision=lax.Precision.HIGHEST
    )
    full_conv = jnp.einsum(
        "kciw,kvw->kciv", partial_conv, right_tabs, precision=lax.Precision.HIGHEST
    )
    return full_conv.reshape(full_conv.shape[0], -1)


def outer_rows(slope, phi):
    return (slope[:, :, None] * phi[:, None, :]).reshape(slope.shape[0], -1)


def solve_step(lower, rhs):
    inner = lax.linalg.triangular_solve(lower, rhs[:, None], left_side=True, lower=True)
    outer = lax.linalg.triangular_solve(lower, inner, left_side=True, lower=True, transpose_a=True)
    return -outer[:, 0]


def on_device(images, gauge_pixel, row_mask, gauge_counts, targets, theta, amplitude, damping):
    ncols = lax.axis_size("cols")
    column = lax.axis_index("cols")
    slots = gauge_pixel.shape[0]
    share = slots // ncols
    channels = theta.shape[0]
    basis_count = theta.shape[1]
    params = channels * basis_count
    local_width = channels // ncols
    own_params = local_width * basis_count
    count = gauge_counts[0]
    live = ((jnp.arange(slots) < count) & (row_mask == 1)).astype(jnp.float32)
    flat_feats = features(images)
    phi = jnp.take(flat_feats, gauge_pixel, axis=1).T
    act = jnp.tanh(jnp.dot(phi, theta.T, precision=lax.Precision.HIGHEST))
    model = jnp.dot(act, amplitude, precision=lax.Precision.HIGHEST)
    resid = live * (model - targets)
    slope = live[:, None] * amplitude[None, :] * (1.0 - act * act)

    def block_rows(values):
        return lax.dynamic_slice_in_dim(values, column * share, share, 0)

    def pick(values):
        return block_rows(values)

    local_slope = lax.dynamic_slice_in_dim(slope, column * local_width, local_width, 1)
    jac_cols = outer_rows(local_slope, phi)
    prefix = jnp.clip(count - column * share, 0, share)
    assigned = lax.all_to_all(jac_cols, "cols", split_axis=0, concat_axis=1, tiled=True)
    assigned_resid = pick(resid)
    trips = (prefix + BLOCK - 1) // BLOCK

    def add_block(which, carry):
        gram = carry[0] + lax.dot_general(
            assigned,
            assigned,
            (((0,), (0,)), ((), ())),
            precision=lax.Precision.HIGHEST,
            preferred_element_type=jnp.float32,
        )
        grad = carry[1] + jnp.dot(assigned_resid, assigned, precision=lax.Precision.HIGHEST)
        return (gram, grad)

    start = (jnp.zeros((params, params), jnp.float32), jnp.zeros((params,), jnp.float32))
    gram_part, grad_part = lax.fori_loop(0, trips, add_block, start)
    live_part = jnp.sum(pick(live))
    gram, grad, total = lax.psum((gram_part, grad_part, live_part), ("rows", "cols"))
    normal = gram / total + damping * jnp.eye(params, dtype=jnp.float32)
    lower = jnp.linalg.cholesky(normal)
    step = solve_step(lower, grad / total)
    local_step = lax.dynamic_slice_in_dim(step, column * own_params, own_params, 0)
    linear_part = lax.psum_scatter(
        jnp.dot(jac_cols, local_step, precision=lax.Precision.HIGHEST),
        "cols",
        scatter_dimension=0,
        tiled=True,
    )
    predicted = block_rows(resid) + linear_part
    return (lower.T, theta + step.reshape(channels, basis_count), predicted)


def solution(mesh):
    return jax.shard_map(
        on_device,
        mesh=mesh,
        in_specs=(P("rows", None, None), P("rows"), P("rows"), P("rows"), P("rows"), P(), P(), P()),
        out_specs=(P(), P(), P(("rows", "cols"))),
        check_vma=False,
    )
```

profile of v0, /device:TPU:1, one launch (start us, length us, event | category | flops | bytes accessed | tf_op | source)
XLA Modules:
  0.0 704.1 jit_solution(6471413244750945603)
XLA Ops:
  7.2 0.6 multiply_reduce_fusion.3
  7.8 0.6 fusion.73
  8.4 0.7 multiply_reduce_fusion.2
  9.1 0.6 multiply_reduce_fusion.1
  10.5 0.6 multiply_reduce_fusion
  11.1 0.7 fusion.50
  11.8 0.7 compare_and_fusion
  16.3 1.0 convolution_bitcast_fusion
  17.3 1.1 fusion.15
  18.4 8.6 %copy.61 = f32[8,8,32,128]{0,3,2,1:T(8,128)} copy(f32[8,8,32,128]{3,2,1,0:T(8,128)S(1)} %fusion.15) | data formatting | bytes 2097152 | tf_op jit(solution)/shard_map/reshape | solution.py:46
  27.0 11.2 %gather_fusion = f32[2048,8]{1,0:T(8,128)S(1)} fusion(f32[8,32768]{0,1:T(8,128)} %bitcast.185, s32[2048]{0:T(1024)S(1)} %fusion.50), kind=kCustom, calls=%fused_computation | custom fusion | bytes 139264 | tf_op jit(solution)/shard_map/jit(_take)/gather | solution.py:72
  38.2 0.3 broadcast_select_fusion
  38.9 1.3 convolution_tanh_fusion
  40.6 1.0 copy.43
  41.5 10.2 %all-to-all-start = ((f32[8,256,64]{1,2,0:T(8,128)}), f32[8,256,64]{1,2,0:T(8,128)S(1)}, u32[]{:S(2)}, u32[]{:S(2)}) async-start(f32[8,256,64]{1,2,0:T(8,128)} %copy.43), calls=%async_computation | async-start | bytes 1048576 | tf_op jit(solution)/shard_map/all_to_all | solution.py:87
  51.8 0.4 fusion.70
  52.1 0.8 dynamic-slice_select_fusion
  52.9 8.2 %all-to-all-done = f32[8,256,64]{1,2,0:T(8,128)S(1)} async-done(((f32[8,256,64]{1,2,0:T(8,128)}), f32[8,256,64]{1,2,0:T(8,128)S(1)}, u32[]{:S(2)}, u32[]{:S(2)}) %all-to-all-start) | async-done | bytes 524320 | tf_op jit(solution)/shard_map/all_to_all | solution.py:87
  61.1 1.0 fusion.83
  62.2 0.5 fusion.84
  62.9 0.3 while.15
  63.2 1.3 copy.45
  64.5 0.7 dynamic-slice_reduce_fusion
  65.9 1.3 dynamic-slice.4
  67.9 104.8 %all-reduce.2 = (f32[]{:T(128)}, f32[512]{0:T(512)S(1)}) all-reduce(f32[]{:T(128)} %dynamic-slice_reduce_fusion, f32[512]{0:T(512)S(1)} %get-tuple-element.82), channel_id=1, replica_groups=mesh['rows'=64,'cols'=8] {'rows','cols'}, use_global_device_ids=true, to_apply=%region_9.0 | all-reduce | flops 513 | bytes 4104 | tf_op jit(solution)/shard_map/psum | solution.py:105
  172.7 0.7 broadcast_divide_fusion
  173.4 363.4 %all-reduce.5.cloned.1.call-done = f32[512,512]{0,1:T(8,128)} async-done(((f32[512,512]{0,1:T(8,128)}), f32[512,512]{0,1:T(8,128)}) %all-reduce.5.cloned.1.call-update) | async-done | bytes 1048592 | tf_op jit(solution)/shard_map/psum | solution.py:105
  536.8 2.0 select_add_fusion
  538.8 0.3 copy.46
  539.1 2.1 fusion.12
  541.3 11.7 %cholesky.103 = f32[128,128]{1,0:T(8,128)S(1)} custom-call(f32[128,128]{1,0:T(8,128)S(1)} %cholesky.263), custom_call_target="Cholesky" | custom-call | tf_op jit(solution)/shard_map/jit(cholesky)/cholesky | solution.py:107
  553.0 9.8 %custom-call.32 = f32[1,128,128]{1,2,0:T(8,128)S(1)} custom-call(f32[1,128,128]{2,1,0:T(8,128)S(1)} %get-tuple-element.162), custom_call_target="InvertDiagBlocksLowerTriangular" | custom-call | tf_op jit(solution)/shard_map/jit(cholesky)/cholesky | solution.py:107
  563.2 0.3 convolution_subtract_fusion
  563.5 11.7 %cholesky.215 = f32[128,128]{1,0:T(8,128)S(1)} custom-call(f32[128,128]{1,0:T(8,128)S(1)} %cholesky.267), custom_call_target="Cholesky" | custom-call | tf_op jit(solution)/shard_map/jit(cholesky)/cholesky | solution.py:107
  575.7 10.0 %custom-call.33 = f32[1,128,128]{1,2,0:T(8,128)S(1)} custom-call(f32[1,128,128]{2,1,0:T(8,128)S(1)} %get-tuple-element.160), custom_call_target="InvertDiagBlocksLowerTriangular" | custom-call | tf_op jit(solution)/shard_map/jit(cholesky)/cholesky | solution.py:107
  586.1 0.6 convolution_subtract_fusion.1
  586.7 11.7 %cholesky.236 = f32[128,128]{1,0:T(8,128)S(1)} custom-call(f32[128,128]{1,0:T(8,128)S(1)} %cholesky.272), custom_call_target="Cholesky" | custom-call | tf_op jit(solution)/shard_map/jit(cholesky)/cholesky | solution.py:107
  598.6 9.8 %custom-call.34 = f32[1,128,128]{1,2,0:T(8,128)S(1)} custom-call(f32[1,128,128]{2,1,0:T(8,128)S(1)} %get-tuple-element.158), custom_call_target="InvertDiagBlocksLowerTriangular" | custom-call | tf_op jit(solution)/shard_map/jit(cholesky)/cholesky | solution.py:107
  608.7 0.5 convolution_subtract_fusion.2
  609.2 11.9 %cholesky.253 = f32[128,128]{1,0:T(8,128)S(1)} custom-call(f32[128,128]{1,0:T(8,128)S(1)} %convolution_subtract_fusion.2), custom_call_target="Cholesky" | custom-call | tf_op jit(solution)/shard_map/jit(cholesky)/cholesky | solution.py:107
  621.3 0.7 compare_reduce_fusion.1
  622.0 0.6 compare_reduce_fusion
  622.6 0.6 compare_reduce_fusion.2
  625.8 1.2 fusion.13
  627.0 11.3 %while.16 = (s32[]{:T(128)}, f32[512,512]{0,1:T(8,128)S(1)}, s32[4,2]{0,1:T(2,128)S(1)}, f32[4,128,128]{2,1,0:T(8,128)}, s32[]{:T(128)}) while((s32[]{:T(128)}, f32[512,512]{0,1:T(8,128)S(1)}, s32[4,2]{0,1:T(2,128)S(1)}, f32[4,128,128]{2,1,0:T(8,128)}, s32[]{:T(128)}) %tuple.61), condition=%wide.while_cond, body=%wide.while_body.sunk | while | flops 2 | bytes 393829 | solution.py:55
  627.1 0.6 fusion.103
  627.7 1.4 dynamic-slice.12
  629.2 0.6 bitcast_dynamic-update-slice_fusion.2
  629.9 0.6 fusion.103
  630.5 1.4 dynamic-slice.12
  632.1 0.6 bitcast_dynamic-update-slice_fusion.2
  632.8 0.6 fusion.103
  633.4 1.4 dynamic-slice.12
  634.9 0.6 bitcast_dynamic-update-slice_fusion.2
  635.6 0.6 fusion.103
  636.2 1.4 dynamic-slice.12
  637.7 0.6 bitcast_dynamic-update-slice_fusion.2
  638.3 40.1 %custom-call.35 = f32[4,128,128]{1,2,0:T(8,128)S(1)} custom-call(f32[4,128,128]{2,1,0:T(8,128)} %get-tuple-element.90), custom_call_target="InvertDiagBlocksLowerTriangular" | custom-call | tf_op jit(solution)/shard_map/triangular_solve | solution.py:55
  681.4 0.6 broadcast.613
  681.9 0.7 fusion.79
  682.6 0.4 fusion.17
  683.0 12.3 %all-reduce.1 = f32[2048]{0:T(1024)S(1)} all-reduce(f32[2048]{0:T(1024)S(1)} %bitcast.197), channel_id=2, replica_groups=mesh['rows'=64,'cols'=8] {'cols'}, use_global_device_ids=true, to_apply=%region_19.20.clone | all-reduce | flops 2048 | bytes 16384
  695.5 0.7 copy.56
  696.1 0.6 dynamic-slice_add_fusion
  (84 shorter events, 7.0 us)
Async XLA Ops:
  7.2 9.1 %copy-start = (f32[8,32,128]{2,1,0:T(8,128)S(1)}, f32[8,32,128]{2,1,0:T(8,128)}, u32[]{:S(2)}) copy-start(f32[8,32,128]{2,1,0:T(8,128)} %param.10) | copy-start | bytes 393220
  7.2 31.7 %copy-start.1 = (f32[64,8]{0,1:T(8,128)S(1)}, f32[64,8]{0,1:T(8,128)}, u32[]{:S(2)}) copy-start(f32[64,8]{0,1:T(8,128)} %param.15) | copy-start | bytes 6148
  7.2 33.0 %copy-start.3 = (f32[64]{0:T(128)S(1)}, f32[64]{0:T(128)}, u32[]{:S(2)}) copy-start(f32[64]{0:T(128)} %param.16) | copy-start | bytes 772
  7.2 33.1 %copy-start.2 = (s32[2048]{0:T(1024)S(1)}, s32[2048]{0:T(1024)}, u32[]{:S(2)}) copy-start(s32[2048]{0:T(1024)} %param.12) | copy-start | bytes 24580
  41.5 19.6 %all-to-all-start = ((f32[8,256,64]{1,2,0:T(8,128)}), f32[8,256,64]{1,2,0:T(8,128)S(1)}, u32[]{:S(2)}, u32[]{:S(2)}) async-start(f32[8,256,64]{1,2,0:T(8,128)} %copy.43), calls=%async_computation | async-start | bytes 1048576 | tf_op jit(solution)/shard_map/all_to_all | solution.py:87
  51.8 485.0 %all-reduce.5.cloned.1.call-start = ((), (), s32[]{:S(2)}) async-start(), calls=%async_computation.1 | async-start | bytes 2097152 | tf_op jit(solution)/shard_map/psum | solution.py:105
Sparse Core Ops, SparseCore 0:
  64.6 472.1 all-reduce.4
where the time goes:
time: 712 us; the launch traced here: 704 us
  waiting for transfers between devices  372 us (52%)
  other arithmetic  133 us (19%)
  blocking collectives  117 us (16%)
  local copies, waits for them, and re-layouts  37.7 us (5%)
  between operations  22.8 us (3%)
  matrix products  10.9 us (2%)
  starting transfers between devices  10.2 us (1%)
    psum x1, waiting for transfers between devices, on_device(): lax.psum((gram_part, grad_part, live_part), ('rows', 'cols'))  363 us
    psum x1, blocking collectives, on_device(): lax.psum((gram_part, grad_part, live_part), ('rows', 'cols'))  105 us
    another operation x14, other arithmetic, on_device(): lower = jnp.linalg.cholesky(normal)  78.8 us
    another operation x3, other arithmetic, solve_step(): lax.linalg.triangular_solve(lower, inner, left_side=True, lower=True, tra...  41.4 us
  transfers between devices with their start and end apart: 2, of which 2 were waited for; matrix products, arithmetic and copies ran while one was open for 1% of the time, Pallas kernels for 0%

commit v1 on v0

v1 whole, which is shorter than its diff:
```python
import functools

import jax
import jax.numpy as jnp
import numpy as np
from jax import lax
from jax.experimental import pallas as pl
from jax.experimental.pallas import tpu as pltpu
from jax.sharding import PartitionSpec as P

HI = lax.Precision.HIGHEST
F32 = jnp.float32
NN = (((1,), (0,)), ((), ()))
NT = (((1,), (1,)), ((), ()))
TN = (((0,), (0,)), ((), ()))
MESH = pl.DeviceIdType.MESH

Y_KIND = [(0, 1.5), (1, 1.5), (0, 1.5), (2, 1.5), (1, 1.5), (0, 1.5), (0, 3.0), (0, 3.0)]
X_KIND = [(0, 1.5), (0, 1.5), (1, 1.5), (0, 1.5), (1, 1.5), (2, 1.5), (0, 3.0), (2, 3.0)]

NB = 128
PARAMS = 512
BLOCKS = [(i, j) for i in range(4) for j in range(i, 4)]
PLANE = 16
ZN = 16
ZROWS = 3
CHUNK = ZN * ZROWS
ROWS = 2 * PLANE * CHUNK
GRAD_ROW = len(BLOCKS) * NB


def dot(a, b, dims):
    return lax.dot_general(a, b, dims, precision=HI, preferred_element_type=F32)


def norm_of(order, width):
    t = np.arange(-12, 13).astype(np.float64)
    e = np.exp(-t * t / (2.0 * width * width))
    if order == 1:
        e = -t / width**2 * e
    if order == 2:
        e = (t * t / width**4 - 1.0 / width**2) * e
    return float(1.0 / np.sqrt(np.sum(e * e)))


def filters(t, kinds):
    t2 = t * t
    env = {w: jnp.exp(t2 * (-1.0 / (2.0 * w * w))) for w in sorted({w for _, w in kinds})}
    out = {}
    for order, w in sorted(set(kinds)):
        scale = norm_of(order, w)
        if order == 0:
            out[order, w] = env[w] * scale
        elif order == 1:
            out[order, w] = t * (-scale / w**2) * env[w]
        else:
            out[order, w] = (t2 * (scale / w**4) - scale / w**2) * env[w]
    return out


def iota(shape, dim):
    return lax.broadcasted_iota(jnp.int32, shape, dim)


def local_kernel(count_ref, img_ref, pix_ref, mask_ref, targ_ref, theta_ref, amp_ref,
                 packed_ref, slope_ref, phi_ref, resid_ref):
    col = lax.axis_index("cols")

    def own(ref):
        v = ref[pl.ds(2 * col, 2), :]
        return jnp.concatenate([v[0:1, :], v[1:2, :]], axis=1)

    pix = own(pix_ref)
    slots = pix.shape[1]
    place = col * slots + iota((1, slots), 1)
    live = ((place < count_ref[0]) & (own(mask_ref) == 1)).astype(F32)

    img = img_ref[...]
    src = iota((img.shape[0], slots), 0)
    row = pix >> 7
    near = (src >> 5) == (row >> 5)
    ty = ((row & 31) - (src & 31)).astype(F32)
    yk = filters(ty, Y_KIND)
    keys = sorted(yk)
    left = jnp.concatenate([jnp.where(near, yk[k], 0.0) for k in keys], axis=1)
    part = dot(img, left, TN)
    tx = ((pix & 127) - iota((img.shape[1], slots), 0)).astype(F32)
    xk = filters(tx, X_KIND)
    phis = []
    for ky, kx in zip(Y_KIND, X_KIND):
        at = keys.index(ky) * slots
        phis.append(jnp.sum(part[:, at:at + slots] * xk[kx], axis=0, keepdims=True))
    phi = jnp.concatenate(phis, axis=0)
    phi_ref[...] = phi

    act = jnp.tanh(dot(theta_ref[...], phi, NN))
    amp = amp_ref[...]
    resid = live * (jnp.sum(amp * act, axis=0, keepdims=True) - own(targ_ref))
    resid_ref[...] = resid
    slope = live * amp * (1.0 - act * act)
    slope_ref[...] = slope
    jac = jnp.concatenate([slope[c:c + 1, :] * phi for c in range(slope.shape[0])], axis=0)

    for i in range(4):
        wide = dot(jac[i * NB:(i + 1) * NB], jac[i * NB:], NT)
        for j in range(i, 4):
            at = BLOCKS.index((i, j)) * NB
            packed_ref[at:at + NB, :] = wide[:, (j - i) * NB:(j - i + 1) * NB]
    grad = dot(jnp.broadcast_to(resid, (8, slots)), jac, NT)
    total = jnp.sum(live, axis=1, keepdims=True)
    rows = [grad[0:1, i * NB:(i + 1) * NB] for i in range(4)]
    rows += [jnp.broadcast_to(total, (1, NB)), jnp.zeros((3, NB), F32)]
    packed_ref[GRAD_ROW:GRAD_ROW + 8, :] = jnp.concatenate(rows, axis=0)
    packed_ref[GRAD_ROW + 8:, :] = jnp.zeros((ROWS - GRAD_ROW - 8, NB), F32)


def reduce_kernel(ysize, x_ref, o_ref, got0, part, got1, zout, got2, zall, full,
                  s0, r0, s1, r1, s2, r2, s3, r3, s4, r4, s5, r5):
    row = lax.axis_index("rows")
    col = lax.axis_index("cols")
    y, z = row // ZN, lax.rem(row, ZN)
    x, core = col // 2, lax.rem(col, 2)
    me = x * ysize + y

    def at_plane(p):
        return {"rows": lax.rem(p, ysize) * ZN + z, "cols": (p // ysize) * 2 + core}

    def at_z(q):
        return {"rows": y * ZN + q, "cols": col}

    partner = {"rows": row, "cols": x * 2 + 1 - core}
    planes = [lax.rem(me + d, PLANE) for d in range(1, PLANE)]
    zs = [lax.rem(z + d, ZN) for d in range(1, ZN)]

    barrier = pltpu.get_barrier_semaphore()
    pl.semaphore_signal(barrier, inc=1, device_id=partner, device_id_type=MESH)
    for p in planes:
        pl.semaphore_signal(barrier, inc=1, device_id=at_plane(p), device_id_type=MESH)
    for q in zs:
        pl.semaphore_signal(barrier, inc=1, device_id=at_z(q), device_id_type=MESH)
    pl.semaphore_wait(barrier, 1 + 2 * 15)

    def copy(src, dst, ssem, rsem, dev):
        return pltpu.make_async_remote_copy(
            src_ref=src, dst_ref=dst, send_sem=ssem, recv_sem=rsem,
            device_id=dev, device_id_type=MESH)

    sends = []

    def start(c):
        c.start()
        sends.append(c)

    order = planes + [me]
    for p in order:
        start(copy(x_ref.at[1 - core, p], got0.at[p], s0.at[p], r0.at[p], partner))
    for d, p in enumerate(order):
        copy(x_ref.at[core, p], got0.at[p], s0.at[p], r0.at[p], partner).wait_recv()
        part[p] = x_ref[core, p] + got0[p]
        if d < PLANE - 1:
            start(copy(part.at[p], got1.at[me], s1.at[p], r1.at[me], at_plane(p)))
    acc = part[me]
    for p in planes:
        copy(part.at[p], got1.at[p], s1.at[p], r1.at[p], at_plane(p)).wait_recv()
        acc = acc + got1[p]
    for q in range(ZN):
        zout[q] = acc[q * ZROWS:(q + 1) * ZROWS, :]
    for q in zs:
        start(copy(zout.at[q], got2.at[z], s2.at[q], r2.at[z], at_z(q)))
    tot = zout[z]
    for q in zs:
        copy(zout.at[q], got2.at[q], s2.at[q], r2.at[q], at_z(q)).wait_recv()
        tot = tot + got2[q]
    zall[z] = tot
    for q in zs:
        start(copy(zall.at[z], zall.at[z], s3.at[q], r3.at[z], at_z(q)))
    for q in zs:
        copy(zall.at[q], zall.at[q], s3.at[q], r3.at[q], at_z(q)).wait_recv()
    full[core, me] = jnp.concatenate([zall[q] for q in range(ZN)], axis=0)
    for p in planes:
        start(copy(full.at[core, me], full.at[core, me], s4.at[p], r4.at[me], at_plane(p)))
    start(copy(full.at[core, me], full.at[core, me], s5.at[me], r5.at[me], partner))
    for p in planes:
        copy(full.at[core, p], full.at[core, p], s4.at[p], r4.at[p], at_plane(p)).wait_recv()
        start(copy(full.at[core, p], full.at[core, p], s5.at[p], r5.at[p], partner))
    for p in order:
        copy(full.at[1 - core, p], full.at[1 - core, p], s5.at[p], r5.at[p], partner).wait_recv()
    for c in sends:
        c.wait_send()
    o_ref[...] = full[...]


def lane(v, c):
    return jnp.broadcast_to(v[:, c:c + 1], (8, NB))


def sub(v, r):
    return jnp.broadcast_to(v[r:r + 1, :], (8, NB))


def factor_block(a, w):
    n = len(a)
    row8 = iota((8, NB), 0)
    col = iota((8, NB), 1)
    rs, ws = [], []

    def stack(rows):
        out = rows[0]
        for i in range(1, 8):
            out = jnp.where(row8 == i, rows[i], out)
        return out

    for s in range(n):
        base = 8 * s
        cb = [lane(a[s], base + m) for m in range(8)]
        t = [[sub(cb[m], i) if i >= m else None for m in range(8)] for i in range(8)]
        pa = [sub(a[s], i) for i in range(8)]
        pw = [sub(w[s], i) for i in range(8)]
        nxt = [lane(a[s + 1], base + m) for m in range(8)] if s + 1 < n else None
        nx = list(nxt) if nxt is not None else None
        low = [[None] * 8 for _ in range(8)]
        inv = []
        for j in range(8):
            r = lax.rsqrt(t[j][j])
            inv.append(r)
            for i in range(j + 1, 8):
                low[i][j] = t[i][j] * r
            pa[j] = pa[j] * r
            pw[j] = pw[j] * r
            if nx is not None:
                nx[j] = nx[j] * r
            for i in range(j + 1, 8):
                for m in range(j + 1, i + 1):
                    t[i][m] = t[i][m] - low[i][j] * low[m][j]
                pa[i] = pa[i] - low[i][j] * pa[j]
                pw[i] = pw[i] - low[i][j] * pw[j]
                if nx is not None:
                    nx[i] = nx[i] - low[i][j] * nx[j]
        rs.append(jnp.where(col >= row8 + base, stack(pa), 0.0))
        ws.append(stack(pw))
        if s + 1 < n:
            for m in range(8):
                a[s + 1] = a[s + 1] - nx[m] * pa[m]
                w[s + 1] = w[s + 1] - nx[m] * pw[m]
        if s + 2 < n:
            qa, qw = list(pa), list(pw)
            for m in reversed(range(8)):
                for i in range(m + 1, 8):
                    qa[m] = qa[m] - low[i][m] * qa[i]
                    qw[m] = qw[m] - low[i][m] * qw[i]
                qa[m] = qa[m] * inv[m]
                qw[m] = qw[m] * inv[m]
            for u in range(s + 2, n):
                for m in range(8):
                    c = lane(a[u], base + m)
                    if m == 0:
                        da, dw = c * qa[m], c * qw[m]
                    else:
                        da, dw = da + c * qa[m], dw + c * qw[m]
                a[u] = a[u] - da
                w[u] = w[u] - dw
    return rs, ws


def solve_kernel(x_ref, slope_ref, phi_ref, resid_ref, theta_ref, damp_ref,
                 r_ref, theta_out, pred_ref, a_ref, w_ref, g_ref):
    inv_total = 1.0 / x_ref[GRAD_ROW + 4:GRAD_ROW + 5, :]
    eye = (iota((NB, NB), 0) == iota((NB, NB), 1)).astype(F32) * damp_ref[0]
    for k, (i, j) in enumerate(BLOCKS):
        v = x_ref[k * NB:(k + 1) * NB, :] * inv_total
        if i == j:
            v = v + eye
        a_ref[i * NB:(i + 1) * NB, j * NB:(j + 1) * NB] = v
        if i != j:
            r_ref[j * NB:(j + 1) * NB, i * NB:(i + 1) * NB] = jnp.zeros((NB, NB), F32)
    for i in range(4):
        g_ref[i] = jnp.broadcast_to(x_ref[GRAD_ROW + i:GRAD_ROW + i + 1, :] * inv_total, (8, NB))

    def body(b, carry):
        at = pl.multiple_of(b * NB, NB)
        strips = [a_ref[pl.ds(at + 8 * s, 8), pl.ds(at, NB)] for s in range(16)]
        row8, col = iota((8, NB), 0), iota((8, NB), 1)
        ident = [(row8 + 8 * s == col).astype(F32) for s in range(16)]
        rs, ws = factor_block(strips, ident)
        for s in range(16):
            r_ref[pl.ds(at + 8 * s, 8), pl.ds(at, NB)] = rs[s]
            w_ref[b, 8 * s:8 * s + 8, :] = ws[s]
        g_ref[b] = dot(g_ref[b], w_ref[b], NT)
        for k in range(3):
            @pl.when(b == k)
            def _():
                lo, hi = k * NB, (k + 1) * NB
                panel = dot(w_ref[k], a_ref[lo:hi, hi:], NN)
                r_ref[lo:hi, hi:] = panel
                for c in range(k + 1, 4):
                    off = c * NB - hi
                    piece = panel[:, off:off + NB]
                    a_ref[c * NB:(c + 1) * NB, c * NB:] -= dot(piece, panel[:, off:], TN)
                    g_ref[c] = g_ref[c] - dot(g_ref[k], piece, NN)
        return carry

    lax.fori_loop(0, 4, body, 0)
    xs = [None] * 4
    for b in reversed(range(4)):
        z = g_ref[b]
        for c in range(b + 1, 4):
            z = z - dot(xs[c], r_ref[b * NB:(b + 1) * NB, c * NB:(c + 1) * NB], NT)
        xs[b] = dot(z, w_ref[b], NN)
    step_row = -jnp.concatenate(xs, axis=1)[0:1, :]
    chans, basis = theta_ref.shape
    own = (iota((chans, PARAMS), 1) >> 3) == iota((chans, PARAMS), 0)
    pick = ((iota((PARAMS, basis), 0) & 7) == iota((PARAMS, basis), 1)).astype(F32)
    step = dot(jnp.where(own, step_row, 0.0), pick, NN)
    theta_out[...] = theta_ref[...] + step
    moved = dot(step, phi_ref[...], NN)
    pred = resid_ref[...] + jnp.sum(slope_ref[...] * moved, axis=0, keepdims=True)
    pred_ref[...] = jnp.concatenate([pred[:, :NB], pred[:, NB:]], axis=0)


VM = pl.BlockSpec(memory_space=pltpu.VMEM)
SM = pl.BlockSpec(memory_space=pltpu.SMEM)


def sds(*shape):
    return jax.ShapeDtypeStruct(shape, F32)


def local_call(counts, img, pix, mask, targ, theta, amp):
    chans, basis = theta.shape
    slots = 256
    return pl.pallas_call(
        local_kernel,
        name="local",
        out_shape=(sds(ROWS, NB), sds(chans, slots), sds(basis, slots), sds(1, slots)),
        in_specs=[SM] + [VM] * 6,
        out_specs=(VM,) * 4,
    )(counts, img, pix, mask, targ, theta, amp)


def reduce_call(packed, ysize):
    dma = pltpu.SemaphoreType.DMA((16,))
    return pl.pallas_call(
        functools.partial(reduce_kernel, ysize),
        name="reduce",
        out_shape=sds(2, PLANE, CHUNK, NB),
        in_specs=[VM],
        out_specs=VM,
        scratch_shapes=[
            pltpu.VMEM((PLANE, CHUNK, NB), F32),
            pltpu.VMEM((PLANE, CHUNK, NB), F32),
            pltpu.VMEM((PLANE, CHUNK, NB), F32),
            pltpu.VMEM((ZN, ZROWS, NB), F32),
            pltpu.VMEM((ZN, ZROWS, NB), F32),
            pltpu.VMEM((ZN, ZROWS, NB), F32),
            pltpu.VMEM((2, PLANE, CHUNK, NB), F32),
        ] + [dma] * 12,
        compiler_params=pltpu.CompilerParams(collective_id=0, has_side_effects=True),
    )(packed.reshape(2, PLANE, CHUNK, NB))


def solve_call(summed, slope, phi, resid, theta, damping):
    slots = resid.shape[1]
    return pl.pallas_call(
        solve_kernel,
        name="solve",
        out_shape=(sds(PARAMS, PARAMS), sds(*theta.shape), sds(slots // NB, NB)),
        in_specs=[VM] * 5 + [SM],
        out_specs=(VM,) * 3,
        scratch_shapes=[
            pltpu.VMEM((PARAMS, PARAMS), F32),
            pltpu.VMEM((4, NB, NB), F32),
            pltpu.VMEM((4, 8, NB), F32),
        ],
    )(summed, slope, phi, resid, theta, damping)


def on_device(images, gauge_pixel, row_mask, gauge_counts, targets, theta, amplitude, damping):
    def lanes(v):
        return v.reshape(-1, NB)

    packed, slope, phi, resid = local_call(
        gauge_counts, images.reshape(-1, NB), lanes(gauge_pixel), lanes(row_mask),
        lanes(targets), theta, amplitude.reshape(-1, 1))
    summed = reduce_call(packed, 4)
    r, new_theta, pred = solve_call(
        summed.reshape(ROWS, NB), slope, phi, resid, theta, damping.reshape(1))
    return r, new_theta, pred.reshape(-1)


def solution(mesh):
    return jax.shard_map(
        on_device,
        mesh=mesh,
        in_specs=(P("rows", None, None), P("rows"), P("rows"), P("rows"), P("rows"), P(), P(), P()),
        out_specs=(P(), P(), P(("rows", "cols"))),
        check_vma=False,
    )
```

time: 712 us -> 87.7 us (0.12); the launches traced: 704 us -> 87.4 us
  waiting for transfers between devices: 372 us -> 0 us
  other arithmetic: 133 us -> 0 us
  blocking collectives: 117 us -> 0 us
  Pallas kernels: 0 us -> 82 us
  local copies, waits for them, and re-layouts: 37.7 us -> 3.48 us
  between operations: 22.8 us -> 1.94 us
  matrix products: 10.9 us -> 0 us
  starting transfers between devices: 10.2 us -> 0 us
    psum x1 -> x0, waiting for transfers between devices: 363 us -> none  [on_device(): lax.psum((gram_part, grad_part, live_part), ('rows', 'cols'))]
    another operation x19 -> x0, other arithmetic: 120 us -> none  [the longest x14 78.8 us: on_device(): lower = jnp.linalg.cholesky(normal)]
    psum x1 -> x0, blocking collectives: 105 us -> none  [on_device(): lax.psum((gram_part, grad_part, live_part), ('rows', 'cols'))]
    pallas_call x0 -> x3, Pallas kernels: none -> 82 us  [the longest x1 52.1 us: reduce_call(): pl.pallas_call(functools.partial(reduce_kernel, ysize), name='reduce', ou...]
    unnamed x1 -> x0, blocking collectives: 12.3 us -> none
    another operation x34 -> x0, local copies, waits for them, and re-layouts: 11.9 us -> none
    gather x1 -> x0, local copies, waits for them, and re-layouts: 11.2 us -> none  [on_device(): phi = jnp.take(flat_feats, gauge_pixel, axis=1).T]
    all_to_all x1 -> x0, starting transfers between devices: 10.2 us -> none  [on_device(): lax.all_to_all(jac_cols, 'cols', split_axis=0, concat_axis=1, tiled=True)]
  transfers between devices with their start and end apart: 2 -> 0, of which waited for: 2 -> 0; matrix products, arithmetic and copies ran while one was open for 1% -> 0% of each run, Pallas kernels for 0% -> 0%
where the time goes in v1:
time: 87.7 us; the launch traced here: 87.4 us
  Pallas kernels  82 us (94%)
  local copies, waits for them, and re-layouts  3.48 us (4%)
  between operations  1.94 us (2%)
    pallas_call x1, Pallas kernels, reduce_call(): pl.pallas_call(functools.partial(reduce_kernel, ysize), name='reduce', ou...  52.1 us
    pallas_call x1, Pallas kernels, solve_call(): pl.pallas_call(solve_kernel, name='solve', out_shape=(sds(PARAMS, PARAMS)...  25.1 us
    pallas_call x1, Pallas kernels, local_call(): pl.pallas_call(local_kernel, name='local', out_shape=(sds(ROWS, NB), sds(...  4.76 us
    unnamed x6, local copies, waits for them, and re-layouts  2.79 us

profile of v1, /device:TPU:1, one launch (start us, length us, event | category | flops | bytes accessed | tf_op | source)
XLA Modules:
  0.0 87.4 jit_solution(1624253081478231744)
XLA Ops:
  1.9 0.0 copy-start
  1.9 0.7 copy-done
  2.6 0.0 copy-start.1
  2.6 0.7 copy.11.theta_ref
  3.3 0.0 copy-done.1
  3.3 0.7 copy.12.amp_ref
  4.0 4.8 %local.1 = (f32[1536,128]{1,0:T(8,128)}, f32[64,256]{1,0:T(8,128)}, f32[8,256]{1,0:T(8,128)}, f32[1,256]{1,0:T(1,128)}) custom-call(s32[1]{0:T(128)S(6)} %copy.15.count_ref, f32[256,128]{1,0:T(8,128)} %bitcast.12, s32[16,128]{1,0:T(8,128)} %bitcast.13, s32[16,128]{1,0:T(8,128)} %bitcast.14, f32[16,128]{1,0:T(8,128)} %bitcast.15, f32[64,8]{1,0:T(8,128)} %copy.11.theta_ref, ...), custom_call_target="tpu_custom_call" | custom-call | tf_op jit(solution)/shard_map/local/pallas_call | solution.py:331
  8.8 52.1 %reduce.1 = f32[2,16,48,128]{3,2,1,0:T(8,128)} custom-call(f32[2,16,48,128]{3,2,1,0:T(8,128)} %bitcast.11), custom_call_target="tpu_custom_call" | custom-call | tf_op jit(solution)/shard_map/reduce/pallas_call | solution.py:342
  60.9 25.1 %solve.1 = (f32[512,512]{1,0:T(8,128)}, f32[64,8]{1,0:T(8,128)}, f32[2,128]{1,0:T(2,128)}) custom-call(f32[1536,128]{1,0:T(8,128)} %bitcast.10, f32[64,256]{1,0:T(8,128)} %get-tuple-element.11.slope_ref, f32[8,256]{1,0:T(8,128)} %get-tuple-element.12.phi_ref, f32[1,256]{1,0:T(1,128)} %get-tuple-element.13.resid_ref, f32[64,8]{1,0:T(8,128)} %copy.11.theta_ref, ...), custom_call_target="tpu_custom_call" | custom-call | tf_op jit(solution)/shard_map/solve/pallas_call | solution.py:363
  86.0 1.4 %copy.14 = f32[64,8]{0,1:T(8,128)} copy(f32[64,8]{1,0:T(8,128)} %get-tuple-element.18) | data formatting | bytes 4096
Async XLA Ops:
  1.9 0.7 copy-start
  2.6 0.7 copy-start.1

commit v2 on v1

v2 whole, which is shorter than its diff:
```python
import functools

import jax
import jax.numpy as jnp
import numpy as np
from jax import lax
from jax.experimental import pallas as pl
from jax.experimental.pallas import tpu as pltpu
from jax.sharding import PartitionSpec as P

HI = lax.Precision.HIGHEST
F32 = jnp.float32
NN = (((1,), (0,)), ((), ()))
NT = (((1,), (1,)), ((), ()))
TN = (((0,), (0,)), ((), ()))
MESH = pl.DeviceIdType.MESH

Y_KIND = [(0, 1.5), (1, 1.5), (0, 1.5), (2, 1.5), (1, 1.5), (0, 1.5), (0, 3.0), (0, 3.0)]
X_KIND = [(0, 1.5), (0, 1.5), (1, 1.5), (0, 1.5), (1, 1.5), (2, 1.5), (0, 3.0), (2, 3.0)]

NB = 128
PARAMS = 512
BLOCKS = [(i, j) for i in range(4) for j in range(i, 4)]
PLANE = 16
ZN = 16
ZROWS = 3
HALF = ZN // 2
PIECE = HALF * ZROWS
CHUNK = ZN * ZROWS
ROWS = 2 * PLANE * CHUNK
GRAD_ROW = len(BLOCKS) * NB


def dot(a, b, dims):
    return lax.dot_general(a, b, dims, precision=HI, preferred_element_type=F32)


def norm_of(order, width):
    t = np.arange(-12, 13).astype(np.float64)
    e = np.exp(-t * t / (2.0 * width * width))
    if order == 1:
        e = -t / width**2 * e
    if order == 2:
        e = (t * t / width**4 - 1.0 / width**2) * e
    return float(1.0 / np.sqrt(np.sum(e * e)))


def filters(t, kinds):
    t2 = t * t
    env = {w: jnp.exp(t2 * (-1.0 / (2.0 * w * w))) for w in sorted({w for _, w in kinds})}
    out = {}
    for order, w in sorted(set(kinds)):
        scale = norm_of(order, w)
        if order == 0:
            out[order, w] = env[w] * scale
        elif order == 1:
            out[order, w] = t * (-scale / w**2) * env[w]
        else:
            out[order, w] = (t2 * (scale / w**4) - scale / w**2) * env[w]
    return out


def iota(shape, dim):
    return lax.broadcasted_iota(jnp.int32, shape, dim)


def local_terms(count_ref, img_ref, pix_ref, mask_ref, targ_ref, theta_ref, amp_ref,
                slope_ref, phi_ref, resid_ref, packed_ref):
    col = lax.axis_index("cols")

    def own(ref):
        v = ref[pl.ds(2 * col, 2), :]
        return jnp.concatenate([v[0:1, :], v[1:2, :]], axis=1)

    pix = own(pix_ref)
    slots = pix.shape[1]
    place = col * slots + iota((1, slots), 1)
    live = ((place < count_ref[0]) & (own(mask_ref) == 1)).astype(F32)

    img = img_ref[...]
    src = iota((img.shape[0], slots), 0)
    row = pix >> 7
    near = (src >> 5) == (row >> 5)
    ty = ((row & 31) - (src & 31)).astype(F32)
    yk = filters(ty, Y_KIND)
    keys = sorted(yk)
    left = jnp.concatenate([jnp.where(near, yk[k], 0.0) for k in keys], axis=1)
    part = dot(img, left, TN)
    tx = ((pix & 127) - iota((img.shape[1], slots), 0)).astype(F32)
    xk = filters(tx, X_KIND)
    phis = []
    for ky, kx in zip(Y_KIND, X_KIND):
        at = keys.index(ky) * slots
        phis.append(jnp.sum(part[:, at:at + slots] * xk[kx], axis=0, keepdims=True))
    phi = jnp.concatenate(phis, axis=0)
    phi_ref[...] = phi

    act = jnp.tanh(dot(theta_ref[...], phi, TN))
    amp = jnp.transpose(jnp.broadcast_to(amp_ref[...], (NB, amp_ref.shape[1])))[:, 0:1]
    resid = live * (jnp.sum(amp * act, axis=0, keepdims=True) - own(targ_ref))
    resid_ref[...] = resid
    slope = live * amp * (1.0 - act * act)
    slope_ref[...] = slope
    jac = jnp.concatenate([slope[c:c + 1, :] * phi for c in range(slope.shape[0])], axis=0)

    for i in range(4):
        wide = dot(jac[i * NB:(i + 1) * NB], jac[i * NB:], NT)
        for j in range(i, 4):
            at = BLOCKS.index((i, j)) * NB
            packed_ref[at:at + NB, :] = wide[:, (j - i) * NB:(j - i + 1) * NB]
    grad = dot(jnp.broadcast_to(resid, (8, slots)), jac, NT)
    total = jnp.sum(live, axis=1, keepdims=True)
    rows = [grad[0:1, i * NB:(i + 1) * NB] for i in range(4)]
    rows += [jnp.broadcast_to(total, (1, NB)), jnp.zeros((3, NB), F32)]
    packed_ref[GRAD_ROW:GRAD_ROW + 8, :] = jnp.concatenate(rows, axis=0)
    packed_ref[GRAD_ROW + 8:, :] = jnp.zeros((ROWS - GRAD_ROW - 8, NB), F32)


def reduce_kernel(ysize, *refs):
    sum_ref, slope_ref, phi_ref, resid_ref = refs[7:11]
    own, got0, part, got1, zout, got2, zall, full = refs[11:19]
    (s0, r0), (s1, r1), (s2, r2), (s3, r3), (s4, r4), (s5, r5) = zip(refs[19::2], refs[20::2])
    row = lax.axis_index("rows")
    col = lax.axis_index("cols")
    y, z = row // ZN, lax.rem(row, ZN)
    x, core = col // 2, lax.rem(col, 2)
    me = x * ysize + y
    near = z // HALF
    far = 1 - near

    def at_plane(p):
        return {"rows": lax.rem(p, ysize) * ZN + z, "cols": (p // ysize) * 2 + core}

    def at_z(q):
        return {"rows": y * ZN + q, "cols": col}

    partner = {"rows": row, "cols": x * 2 + 1 - core}
    planes = [lax.rem(me + d, PLANE) for d in range(1, PLANE)]
    near_z = [near * HALF + lax.rem(z + d, HALF) for d in range(1, HALF)]
    far_z = [far * HALF + d for d in range(HALF)]

    barrier = pltpu.get_barrier_semaphore()
    for dev in [partner] + [at_plane(p) for p in planes] + [at_z(q) for q in near_z + far_z]:
        pl.semaphore_signal(barrier, inc=1, device_id=dev, device_id_type=MESH)

    local_terms(*refs[:7], slope_ref, phi_ref, resid_ref, own)

    pl.semaphore_wait(barrier, 1 + 2 * 15)

    sends = []

    def copy(src, dst, ssem, rsem, dev):
        return pltpu.make_async_remote_copy(
            src_ref=src, dst_ref=dst, send_sem=ssem, recv_sem=rsem,
            device_id=dev, device_id_type=MESH)

    def start(*args):
        c = copy(*args)
        c.start()
        sends.append(c)

    def rows_of(half_of, p, h):
        return pl.ds(pl.multiple_of((half_of * PLANE + p) * CHUNK + h * PIECE, 8), PIECE)

    order = planes + [me]
    for h in (far, near):
        for p in order:
            start(own.at[rows_of(1 - core, p, h)], got0.at[h, p], s0.at[h, p], r0.at[h, p], partner)
    for h in (far, near):
        for d, p in enumerate(order):
            mine = own.at[rows_of(core, p, h)]
            copy(mine, got0.at[h, p], s0.at[h, p], r0.at[h, p], partner).wait_recv()
            part[h, p] = mine[...] + got0[h, p]
            if d < PLANE - 1:
                start(part.at[h, p], got1.at[h, me], s1.at[h, p], r1.at[h, me], at_plane(p))
    for h, zs in ((far, far_z), (near, near_z)):
        acc = part[h, me]
        for p in planes:
            copy(part.at[h, p], got1.at[h, p], s1.at[h, p], r1.at[h, p], at_plane(p)).wait_recv()
            acc = acc + got1[h, p]
        for q in range(HALF):
            zout[h * HALF + q] = acc[q * ZROWS:(q + 1) * ZROWS, :]
        for q in zs:
            start(zout.at[q], got2.at[z], s2.at[q], r2.at[z], at_z(q))
    tot = zout[z]
    for q in near_z + far_z:
        copy(zout.at[q], got2.at[q], s2.at[q], r2.at[q], at_z(q)).wait_recv()
        tot = tot + got2[q]
    zall[z] = tot
    for q in far_z + near_z:
        start(zall.at[z], zall.at[z], s3.at[q], r3.at[z], at_z(q))
    for h, zs in ((near, near_z), (far, far_z)):
        for q in zs:
            copy(zall.at[q], zall.at[q], s3.at[q], r3.at[q], at_z(q)).wait_recv()
        block = full.at[rows_of(core, me, h)]
        block[...] = jnp.concatenate([zall[h * HALF + q] for q in range(HALF)], axis=0)
        for p in planes:
            start(block, block, s4.at[h, p], r4.at[h, me], at_plane(p))
        start(block, block, s5.at[h, me], r5.at[h, me], partner)
    for h in (near, far):
        for p in planes:
            block = full.at[rows_of(core, p, h)]
            copy(block, block, s4.at[h, p], r4.at[h, p], at_plane(p)).wait_recv()
            start(block, block, s5.at[h, p], r5.at[h, p], partner)
    for h in (near, far):
        for p in order:
            block = full.at[rows_of(1 - core, p, h)]
            copy(block, block, s5.at[h, p], r5.at[h, p], partner).wait_recv()
    for c in sends:
        c.wait_send()
    sum_ref[...] = full[...]


def lane(v, c):
    return jnp.take_along_axis(v, jnp.full((8, NB), c, jnp.int32), axis=1, mode="promise_in_bounds")


def sub(v, r):
    return jnp.broadcast_to(v[r:r + 1, :], (8, NB))


def factor_block(c):
    n = len(c)
    row8 = iota((8, NB), 0)
    col = iota((8, NB), 1)
    ws = []

    for s in range(n):
        base = 8 * s
        tile = (col >= base) & (col < base + 8)
        cb = [lane(c[s], base + m) for m in range(8)]
        t = [[sub(cb[m], i) if i >= m else None for m in range(8)] for i in range(8)]
        own = jnp.where(tile, (row8 + base == col).astype(F32), c[s])
        pa = [sub(own, i) for i in range(8)]
        nx = [lane(c[s + 1], base + m) for m in range(8)] if s + 1 < n else None
        rest = [[lane(c[u], base + m) for m in range(8)] for u in range(s + 2, n)]
        low = [[None] * 8 for _ in range(8)]
        inv = []
        for j in range(0, 8, 2):
            k = j + 1
            a11, a21, a22 = t[j][j], t[k][j], t[k][k]
            det = a11 * a22 - a21 * a21
            r1, r2 = lax.rsqrt(a11), lax.rsqrt(a11 * det)
            g1, g2 = a11 * r2, a21 * r2
            inv += [r1, g1]

            def pair(u, v):
                return u * r1, g1 * v - g2 * u

            low[k][j] = a21 * r1
            for i in range(j + 2, 8):
                low[i][j], low[i][k] = pair(t[i][j], t[i][k])
            for i in range(j + 2, 8):
                for m in range(j + 2, i + 1):
                    t[i][m] = t[i][m] - low[i][j] * low[m][j] - low[i][k] * low[m][k]
            rows = [pa] if nx is None else [pa, nx]
            for v in rows:
                v[j], v[k] = pair(v[j], v[k])
                for i in range(j + 2, 8):
                    v[i] = v[i] - low[i][j] * v[j] - low[i][k] * v[k]
        if s + 1 < n:
            d = [nx[m] * pa[m] for m in range(8)]
            d = ((d[0] + d[1]) + (d[2] + d[3])) + ((d[4] + d[5]) + (d[6] + d[7]))
            c[s + 1] = jnp.where(tile, 0.0, c[s + 1]) - d
        out = pa[0]
        for i in range(1, 8):
            out = jnp.where(row8 == i, pa[i], out)
        ws.append(jnp.where(col < base + 8, out, 0.0))
        if s + 2 < n:
            q = list(pa)
            for m in reversed(range(8)):
                for i in range(m + 1, 8):
                    q[m] = q[m] - low[i][m] * q[i]
                q[m] = q[m] * inv[m]
            for u in range(s + 2, n):
                cu = jnp.where(tile, 0.0, c[u])
                for m in range(8):
                    cu = cu - rest[u - s - 2][m] * q[m]
                c[u] = cu
    return ws


def solve_kernel(x_ref, slope_ref, phi_ref, resid_ref, theta_ref, damp_ref,
                 r_ref, theta_out, pred_ref, a_ref, w_ref, g_ref, y_ref):
    inv_total = 1.0 / x_ref[GRAD_ROW + 4:GRAD_ROW + 5, :]
    eye = (iota((NB, NB), 0) == iota((NB, NB), 1)).astype(F32) * damp_ref[0]
    upper = iota((NB, NB), 0) <= iota((NB, NB), 1)
    for k, (i, j) in enumerate(BLOCKS):
        v = x_ref[k * NB:(k + 1) * NB, :] * inv_total
        if i == j:
            v = v + eye
        else:
            r_ref[j * NB:(j + 1) * NB, i * NB:(i + 1) * NB] = jnp.zeros((NB, NB), F32)
        a_ref[i * NB:(i + 1) * NB, j * NB:(j + 1) * NB] = v
    for i in range(4):
        g_ref[i] = x_ref[GRAD_ROW + i:GRAD_ROW + i + 1, :] * inv_total

    def body(b, carry):
        at = pl.multiple_of(b * NB, NB)
        ws = factor_block([a_ref[pl.ds(at + 8 * s, 8), pl.ds(at, NB)] for s in range(16)])
        for s in range(16):
            w_ref[b, 8 * s:8 * s + 8, :] = ws[s]
        for k in range(4):
            @pl.when(b == k)
            def _():
                lo, hi = k * NB, (k + 1) * NB
                w = w_ref[k]
                panel = dot(w, a_ref[lo:hi, lo:], NN)
                r_ref[lo:hi, lo:hi] = jnp.where(upper, panel[:, :NB], 0.0)
                y = jnp.sum(w * g_ref[k], axis=1, keepdims=True)
                y_ref[k] = y
                if k < 3:
                    r_ref[lo:hi, hi:] = panel[:, NB:]
                for c in range(k + 1, 4):
                    off = c * NB - lo
                    piece = panel[:, off:off + NB]
                    a_ref[c * NB:(c + 1) * NB, c * NB:] -= dot(piece, panel[:, off:], TN)
                    g_ref[c] = g_ref[c] - jnp.sum(piece * y, axis=0, keepdims=True)
        return carry

    lax.fori_loop(0, 4, body, 0)
    xs = [None] * 4
    for b in reversed(range(4)):
        z = y_ref[b]
        if b < 3:
            d = r_ref[b * NB:(b + 1) * NB, (b + 1) * NB:(b + 2) * NB] * xs[b + 1]
            for c in range(b + 2, 4):
                d = d + r_ref[b * NB:(b + 1) * NB, c * NB:(c + 1) * NB] * xs[c]
            z = z - jnp.sum(d, axis=1, keepdims=True)
        xs[b] = jnp.sum(w_ref[b] * z, axis=0, keepdims=True)
    step_row = -jnp.concatenate(xs, axis=1)
    basis, chans = theta_ref.shape
    own = (iota((basis, PARAMS), 1) & 7) == iota((basis, PARAMS), 0)
    pick = ((iota((PARAMS, chans), 0) >> 3) == iota((PARAMS, chans), 1)).astype(F32)
    step = dot(jnp.where(own, step_row, 0.0), pick, NN)
    theta_out[...] = theta_ref[...] + step
    moved = dot(step, phi_ref[...], TN)
    pred = resid_ref[...] + jnp.sum(slope_ref[...] * moved, axis=0, keepdims=True)
    pred_ref[...] = jnp.concatenate([pred[:, :NB], pred[:, NB:]], axis=0)


THETA_T = True
VM = pl.BlockSpec(memory_space=pltpu.VMEM)
SM = pl.BlockSpec(memory_space=pltpu.SMEM)


def sds(*shape):
    return jax.ShapeDtypeStruct(shape, F32)


def reduce_call(ysize, *args):
    basis, chans = args[5].shape
    slots = 256
    pair, line = pltpu.SemaphoreType.DMA((2, PLANE)), pltpu.SemaphoreType.DMA((ZN,))
    return pl.pallas_call(
        functools.partial(reduce_kernel, ysize),
        name="reduce",
        out_shape=(sds(ROWS, NB), sds(chans, slots), sds(basis, slots), sds(1, slots)),
        in_specs=[SM] + [VM] * 6,
        out_specs=(VM,) * 4,
        scratch_shapes=[
            pltpu.VMEM((ROWS, NB), F32),
            pltpu.VMEM((2, PLANE, PIECE, NB), F32),
            pltpu.VMEM((2, PLANE, PIECE, NB), F32),
            pltpu.VMEM((2, PLANE, PIECE, NB), F32),
            pltpu.VMEM((ZN, ZROWS, NB), F32),
            pltpu.VMEM((ZN, ZROWS, NB), F32),
            pltpu.VMEM((ZN, ZROWS, NB), F32),
            pltpu.VMEM((ROWS, NB), F32),
        ] + [pair] * 4 + [line] * 4 + [pair] * 4,
        compiler_params=pltpu.CompilerParams(collective_id=0, has_side_effects=True),
    )(*args)


def solve_call(summed, slope, phi, resid, theta, damping):
    slots = resid.shape[1]
    return pl.pallas_call(
        solve_kernel,
        name="solve",
        out_shape=(sds(PARAMS, PARAMS), sds(*theta.shape), sds(slots // NB, NB)),
        in_specs=[VM] * 5 + [SM],
        out_specs=(VM,) * 3,
        scratch_shapes=[
            pltpu.VMEM((PARAMS, PARAMS), F32),
            pltpu.VMEM((4, NB, NB), F32),
            pltpu.VMEM((4, 1, NB), F32),
            pltpu.VMEM((4, NB, 1), F32),
        ],
    )(summed, slope, phi, resid, theta, damping)


def on_device(images, gauge_pixel, row_mask, gauge_counts, targets, theta, amplitude, damping):
    def lanes(v):
        return v.reshape(-1, NB)

    summed, slope, phi, resid = reduce_call(
        4, gauge_counts, images.reshape(-1, NB), lanes(gauge_pixel), lanes(row_mask),
        lanes(targets), theta.T, amplitude.reshape(1, -1))
    r, new_theta, pred = solve_call(
        summed, slope, phi, resid, theta.T, damping.reshape(1))
    return r, new_theta.T, pred.reshape(-1)


def solution(mesh):
    return jax.shard_map(
        on_device,
        mesh=mesh,
        in_specs=(P("rows", None, None), P("rows"), P("rows"), P("rows"), P("rows"), P(), P(), P()),
        out_specs=(P(), P(), P(("rows", "cols"))),
        check_vma=False,
    )
```

time: 87.7 us -> 70 us (0.80)
  Pallas kernels: 82 us -> 67.9 us
  local copies, waits for them, and re-layouts: 3.48 us -> 0 us
    pallas_call x1, Pallas kernels: 25.1 us -> 17.1 us  [solve_call(): pl.pallas_call(solve_kernel, name='solve', out_shape=(sds(PARAMS, PARAMS)...]
    pallas_call x1 -> x0, Pallas kernels: 4.76 us -> none  [local_call(): pl.pallas_call(local_kernel, name='local', out_shape=(sds(ROWS, NB), sds(...]
    unnamed x6 -> x0, local copies, waits for them, and re-layouts: 2.79 us -> none
    pallas_call x1, Pallas kernels: 52.1 us -> 50.8 us  [reduce_call(): pl.pallas_call(functools.partial(reduce_kernel, ysize), name='reduce', ou...]
where the time goes in v2:
time: 70 us; the launch traced here: 69.8 us
  Pallas kernels  67.9 us (97%)
  between operations  1.93 us (3%)
    pallas_call x1, Pallas kernels, reduce_call(): pl.pallas_call(functools.partial(reduce_kernel, ysize), name='reduce', ou...  50.8 us
    pallas_call x1, Pallas kernels, solve_call(): pl.pallas_call(solve_kernel, name='solve', out_shape=(sds(PARAMS, PARAMS)...  17.1 us

profile of v2, /device:TPU:1, one launch (start us, length us, event | category | flops | bytes accessed | tf_op | source)
XLA Modules:
  0.0 69.8 jit_solution(3597059400483017789)
XLA Ops:
  1.9 50.8 %reduce.1 = (f32[1536,128]{1,0:T(8,128)}, f32[64,256]{1,0:T(8,128)}, f32[8,256]{1,0:T(8,128)}, f32[1,256]{1,0:T(1,128)}) custom-call(s32[1]{0:T(128)S(6)} %copy.11.refs_0_, f32[256,128]{1,0:T(8,128)} %bitcast.10, s32[16,128]{1,0:T(8,128)} %bitcast.13, s32[16,128]{1,0:T(8,128)} %bitcast.14, f32[16,128]{1,0:T(8,128)} %bitcast.15, f32[8,64]{1,0:T(8,128)} %bitcast.11, ...), custom_call_target="tpu_custom_call" | custom-call | tf_op jit(solution)/shard_map/reduce/pallas_call | solution.py:355
  52.7 17.1 %solve.1 = (f32[512,512]{1,0:T(8,128)}, f32[8,64]{1,0:T(8,128)}, f32[2,128]{1,0:T(2,128)}) custom-call(f32[1536,128]{1,0:T(8,128)} %get-tuple-element.10.x_ref, f32[64,256]{1,0:T(8,128)} %get-tuple-element.11.slope_ref, f32[8,256]{1,0:T(8,128)} %get-tuple-element.12.phi_ref, f32[1,256]{1,0:T(1,128)} %get-tuple-element.13.resid_ref, f32[8,64]{1,0:T(8,128)} %bitcast.12, ...), custom_call_target="tpu_custom_call" | custom-call | tf_op jit(solution)/shard_map/solve/pallas_call | solution.py:377

commit v3 on v2

--- a/solution.py
+++ b/solution.py
@@ -20,15 +20,12 @@
 
 NB = 128
 PARAMS = 512
-BLOCKS = [(i, j) for i in range(4) for j in range(i, 4)]
+BLOCKS = [(0, 0), (0, 1), (0, 2), (0, 3), (1, 2), (1, 3), (2, 2), (2, 3)]
 PLANE = 16
 ZN = 16
-ZROWS = 3
-HALF = ZN // 2
-PIECE = HALF * ZROWS
-CHUNK = ZN * ZROWS
-ROWS = 2 * PLANE * CHUNK
-GRAD_ROW = len(BLOCKS) * NB
+QUARTERS = 4
+ROWS = len(BLOCKS) * NB
+EXTRA = 8
 
 
 def dot(a, b, dims):
@@ -103,30 +100,40 @@
     slope_ref[...] = slope
     jac = jnp.concatenate([slope[c:c + 1, :] * phi for c in range(slope.shape[0])], axis=0)
 
+    upper = iota((NB, NB), 0) <= iota((NB, NB), 1)
+    diag = iota((NB, NB), 0) == iota((NB, NB), 1)
+    rows = []
     for i in range(4):
         wide = dot(jac[i * NB:(i + 1) * NB], jac[i * NB:], NT)
         for j in range(i, 4):
-            at = BLOCKS.index((i, j)) * NB
-            packed_ref[at:at + NB, :] = wide[:, (j - i) * NB:(j - i + 1) * NB]
+            block = wide[:, (j - i) * NB:(j - i + 1) * NB]
+            if i == j and i % 2 == 0:
+                first = block
+                continue
+            at = BLOCKS.index((i - 1, i - 1) if i == j else (i, j)) * NB
+            if i == j:
+                rows.append(jnp.sum(jnp.where(diag, block, 0.0), axis=0, keepdims=True))
+                block = jnp.where(upper, first, block)
+            packed_ref[at:at + NB, :] = block
     grad = dot(jnp.broadcast_to(resid, (8, slots)), jac, NT)
     total = jnp.sum(live, axis=1, keepdims=True)
-    rows = [grad[0:1, i * NB:(i + 1) * NB] for i in range(4)]
-    rows += [jnp.broadcast_to(total, (1, NB)), jnp.zeros((3, NB), F32)]
-    packed_ref[GRAD_ROW:GRAD_ROW + 8, :] = jnp.concatenate(rows, axis=0)
-    packed_ref[GRAD_ROW + 8:, :] = jnp.zeros((ROWS - GRAD_ROW - 8, NB), F32)
+    rows = [grad[0:1, i * NB:(i + 1) * NB] for i in range(4)] + rows
+    rows += [jnp.broadcast_to(total, (1, NB)), jnp.zeros((1, NB), F32)]
+    return jnp.concatenate(rows, axis=0)
 
 
 def reduce_kernel(ysize, *refs):
     sum_ref, slope_ref, phi_ref, resid_ref = refs[7:11]
-    own, got0, part, got1, zout, got2, zall, full = refs[11:19]
-    (s0, r0), (s1, r1), (s2, r2), (s3, r3), (s4, r4), (s5, r5) = zip(refs[19::2], refs[20::2])
+    own, got0, part, got1, zout, got2, zall, full, e0, e1, e2 = refs[11:22]
+    (s0, r0), (s1, r1), (s2, r2), (s3, r3), (s4, r4), (s5, r5) = zip(refs[22:34:2], refs[23:34:2])
+    (t0, v0), (t1, v1), (t2, v2) = zip(refs[34::2], refs[35::2])
     row = lax.axis_index("rows")
     col = lax.axis_index("cols")
     y, z = row // ZN, lax.rem(row, ZN)
     x, core = col // 2, lax.rem(col, 2)
     me = x * ysize + y
-    near = z // HALF
-    far = 1 - near
+    near = z // QUARTERS
+    far_first = [lax.rem(near + d, QUARTERS) for d in (2, 1, 3, 0)]
 
     def at_plane(p):
         return {"rows": lax.rem(p, ysize) * ZN + z, "cols": (p // ysize) * 2 + core}
@@ -136,14 +143,15 @@
 
     partner = {"rows": row, "cols": x * 2 + 1 - core}
     planes = [lax.rem(me + d, PLANE) for d in range(1, PLANE)]
-    near_z = [near * HALF + lax.rem(z + d, HALF) for d in range(1, HALF)]
-    far_z = [far * HALF + d for d in range(HALF)]
+    peers = [[k * 4 + d for d in range(4)] for k in far_first[:3]]
+    peers.append([near * 4 + lax.rem(z + d, 4) for d in range(1, 4)])
+    zs = [q for group in peers for q in group]
 
     barrier = pltpu.get_barrier_semaphore()
-    for dev in [partner] + [at_plane(p) for p in planes] + [at_z(q) for q in near_z + far_z]:
+    for dev in [partner] + [at_plane(p) for p in planes] + [at_z(q) for q in zs]:
         pl.semaphore_signal(barrier, inc=1, device_id=dev, device_id_type=MESH)
 
-    local_terms(*refs[:7], slope_ref, phi_ref, resid_ref, own)
+    e0[core] = local_terms(*refs[:7], slope_ref, phi_ref, resid_ref, own)
 
     pl.semaphore_wait(barrier, 1 + 2 * 15)
 
@@ -159,56 +167,78 @@
         c.start()
         sends.append(c)
 
-    def rows_of(half_of, p, h):
-        return pl.ds(pl.multiple_of((half_of * PLANE + p) * CHUNK + h * PIECE, 8), PIECE)
-
-    order = planes + [me]
-    for h in (far, near):
-        for p in order:
-            start(own.at[rows_of(1 - core, p, h)], got0.at[h, p], s0.at[h, p], r0.at[h, p], partner)
-    for h in (far, near):
-        for d, p in enumerate(order):
-            mine = own.at[rows_of(core, p, h)]
-            copy(mine, got0.at[h, p], s0.at[h, p], r0.at[h, p], partner).wait_recv()
-            part[h, p] = mine[...] + got0[h, p]
-            if d < PLANE - 1:
-                start(part.at[h, p], got1.at[h, me], s1.at[h, p], r1.at[h, me], at_plane(p))
-    for h, zs in ((far, far_z), (near, near_z)):
-        acc = part[h, me]
+    def block(half, k):
+        return pl.ds(pl.multiple_of((half * QUARTERS + k) * NB, NB), NB)
+
+    def tile(p):
+        return pl.ds(pl.multiple_of(p * 8, 8), 8)
+
+    def tile_of(half, k, p):
+        return pl.ds(pl.multiple_of((half * QUARTERS + k) * NB + p * 8, 8), 8)
+
+    for k in far_first:
+        start(own.at[block(1 - core, k)], got0.at[k], s0.at[k], r0.at[k], partner)
+    start(e0.at[core], e0.at[core], t0, v0, partner)
+    for k in far_first:
+        mine = own.at[block(core, k)]
+        copy(mine, got0.at[k], s0.at[k], r0.at[k], partner).wait_recv()
+        part[k] = mine[...] + got0[k]
         for p in planes:
-            copy(part.at[h, p], got1.at[h, p], s1.at[h, p], r1.at[h, p], at_plane(p)).wait_recv()
-            acc = acc + got1[h, p]
-        for q in range(HALF):
-            zout[h * HALF + q] = acc[q * ZROWS:(q + 1) * ZROWS, :]
-        for q in zs:
+            start(part.at[k, tile(p)], got1.at[k, me], s1.at[k, p], r1.at[k, me], at_plane(p))
+    copy(e0.at[1 - core], e0.at[1 - core], t0, v0, partner).wait_recv()
+    e1[me] = e0[0] + e0[1]
+    for p in planes:
+        start(e1.at[me], e1.at[me], t1.at[p], v1.at[me], at_plane(p))
+    for k, group in zip(far_first, peers):
+        acc = part[k, tile(me)]
+        for p in planes:
+            copy(part.at[k, tile(p)], got1.at[k, p], s1.at[k, p], r1.at[k, p], at_plane(p)).wait_recv()
+            acc = acc + got1[k, p]
+        for d in range(4):
+            zout[k * 4 + d] = acc[2 * d:2 * d + 2, :]
+        for q in group:
             start(zout.at[q], got2.at[z], s2.at[q], r2.at[z], at_z(q))
+    for p in planes:
+        copy(e1.at[p], e1.at[p], t1.at[p], v1.at[p], at_plane(p)).wait_recv()
+    acc = e1[0]
+    for p in range(1, PLANE):
+        acc = acc + e1[p]
+    e2[z] = acc
+    for q in zs:
+        start(e2.at[z], e2.at[z], t2.at[q], v2.at[z], at_z(q))
     tot = zout[z]
-    for q in near_z + far_z:
+    for q in reversed(zs):
         copy(zout.at[q], got2.at[q], s2.at[q], r2.at[q], at_z(q)).wait_recv()
         tot = tot + got2[q]
     zall[z] = tot
-    for q in far_z + near_z:
+    for q in zs:
         start(zall.at[z], zall.at[z], s3.at[q], r3.at[z], at_z(q))
-    for h, zs in ((near, near_z), (far, far_z)):
-        for q in zs:
+    near_first = list(reversed(far_first))
+    for k, group in zip(near_first, reversed(peers)):
+        for q in group:
             copy(zall.at[q], zall.at[q], s3.at[q], r3.at[q], at_z(q)).wait_recv()
-        block = full.at[rows_of(core, me, h)]
-        block[...] = jnp.concatenate([zall[h * HALF + q] for q in range(HALF)], axis=0)
+        mine = full.at[tile_of(core, k, me)]
+        mine[...] = jnp.concatenate([zall[k * 4 + d] for d in range(4)], axis=0)
         for p in planes:
-            start(block, block, s4.at[h, p], r4.at[h, me], at_plane(p))
-        start(block, block, s5.at[h, me], r5.at[h, me], partner)
-    for h in (near, far):
+            start(mine, mine, s4.at[k, p], r4.at[k, me], at_plane(p))
+    for q in zs:
+        copy(e2.at[q], e2.at[q], t2.at[q], v2.at[q], at_z(q)).wait_recv()
+    acc = e2[0]
+    for q in range(1, ZN):
+        acc = acc + e2[q]
+    sum_ref[ROWS:ROWS + EXTRA, :] = acc
+    for k in near_first:
         for p in planes:
-            block = full.at[rows_of(core, p, h)]
-            copy(block, block, s4.at[h, p], r4.at[h, p], at_plane(p)).wait_recv()
-            start(block, block, s5.at[h, p], r5.at[h, p], partner)
-    for h in (near, far):
-        for p in order:
-            block = full.at[rows_of(1 - core, p, h)]
-            copy(block, block, s5.at[h, p], r5.at[h, p], partner).wait_recv()
+            got = full.at[tile_of(core, k, p)]
+            copy(got, got, s4.at[k, p], r4.at[k, p], at_plane(p)).wait_recv()
+        mine = full.at[block(core, k)]
+        start(mine, mine, s5.at[k], r5.at[k], partner)
+    for k in near_first:
+        got = full.at[block(1 - core, k)]
+        copy(got, got, s5.at[k], r5.at[k], partner).wait_recv()
     for c in sends:
         c.wait_send()
-    sum_ref[...] = full[...]
+    sum_ref[0:ROWS, :] = full[...]
 
 
 def lane(v, c):
@@ -282,18 +312,26 @@
 
 def solve_kernel(x_ref, slope_ref, phi_ref, resid_ref, theta_ref, damp_ref,
                  r_ref, theta_out, pred_ref, a_ref, w_ref, g_ref, y_ref):
-    inv_total = 1.0 / x_ref[GRAD_ROW + 4:GRAD_ROW + 5, :]
-    eye = (iota((NB, NB), 0) == iota((NB, NB), 1)).astype(F32) * damp_ref[0]
+    inv_total = 1.0 / x_ref[ROWS + 6:ROWS + 7, :]
+    same = iota((NB, NB), 0) == iota((NB, NB), 1)
+    eye = same.astype(F32) * damp_ref[0]
     upper = iota((NB, NB), 0) <= iota((NB, NB), 1)
     for k, (i, j) in enumerate(BLOCKS):
         v = x_ref[k * NB:(k + 1) * NB, :] * inv_total
         if i == j:
-            v = v + eye
+            t = jnp.transpose(v)
+            low = jnp.where(upper, t, v)
+            row = ROWS + 4 + i // 2
+            low = jnp.where(same, x_ref[row:row + 1, :] * inv_total, low)
+            a_ref[i * NB:(i + 1) * NB, i * NB:(i + 1) * NB] = jnp.where(upper, v, t) + eye
+            i, v = i + 1, low + eye
+            a_ref[i * NB:(i + 1) * NB, i * NB:(i + 1) * NB] = v
         else:
-            r_ref[j * NB:(j + 1) * NB, i * NB:(i + 1) * NB] = jnp.zeros((NB, NB), F32)
-        a_ref[i * NB:(i + 1) * NB, j * NB:(j + 1) * NB] = v
+            a_ref[i * NB:(i + 1) * NB, j * NB:(j + 1) * NB] = v
     for i in range(4):
-        g_ref[i] = x_ref[GRAD_ROW + i:GRAD_ROW + i + 1, :] * inv_total
+        for j in range(i):
+            r_ref[i * NB:(i + 1) * NB, j * NB:(j + 1) * NB] = jnp.zeros((NB, NB), F32)
+        g_ref[i] = x_ref[ROWS + i:ROWS + i + 1, :] * inv_total
 
     def body(b, carry):
         at = pl.multiple_of(b * NB, NB)
@@ -351,23 +389,27 @@
 def reduce_call(ysize, *args):
     basis, chans = args[5].shape
     slots = 256
-    pair, line = pltpu.SemaphoreType.DMA((2, PLANE)), pltpu.SemaphoreType.DMA((ZN,))
+    dma = pltpu.SemaphoreType.DMA
+    four, grid, line = dma((QUARTERS,)), dma((QUARTERS, PLANE)), dma((ZN,))
     return pl.pallas_call(
         functools.partial(reduce_kernel, ysize),
         name="reduce",
-        out_shape=(sds(ROWS, NB), sds(chans, slots), sds(basis, slots), sds(1, slots)),
+        out_shape=(sds(ROWS + EXTRA, NB), sds(chans, slots), sds(basis, slots), sds(1, slots)),
         in_specs=[SM] + [VM] * 6,
         out_specs=(VM,) * 4,
         scratch_shapes=[
             pltpu.VMEM((ROWS, NB), F32),
-            pltpu.VMEM((2, PLANE, PIECE, NB), F32),
-            pltpu.VMEM((2, PLANE, PIECE, NB), F32),
-            pltpu.VMEM((2, PLANE, PIECE, NB), F32),
-            pltpu.VMEM((ZN, ZROWS, NB), F32),
-            pltpu.VMEM((ZN, ZROWS, NB), F32),
-            pltpu.VMEM((ZN, ZROWS, NB), F32),
+            pltpu.VMEM((QUARTERS, NB, NB), F32),
+            pltpu.VMEM((QUARTERS, NB, NB), F32),
+            pltpu.VMEM((QUARTERS, PLANE, 8, NB), F32),
+            pltpu.VMEM((ZN, 2, NB), F32),
+            pltpu.VMEM((ZN, 2, NB), F32),
+            pltpu.VMEM((ZN, 2, NB), F32),
             pltpu.VMEM((ROWS, NB), F32),
-        ] + [pair] * 4 + [line] * 4 + [pair] * 4,
+            pltpu.VMEM((2, 8, NB), F32),
+            pltpu.VMEM((PLANE, 8, NB), F32),
+            pltpu.VMEM((ZN, 8, NB), F32),
+        ] + [four] * 2 + [grid] * 2 + [line] * 4 + [grid] * 2 + [four] * 2 + [dma] * 2 + [line] * 4,
         compiler_params=pltpu.CompilerParams(collective_id=0, has_side_effects=True),
     )(*args)
 

time: 70 us -> 67.2 us (0.960)
  Pallas kernels: 67.9 us -> 65.1 us
    pallas_call x1, Pallas kernels: 50.8 us -> 48.1 us  [reduce_call(): pl.pallas_call(functools.partial(reduce_kernel, ysize), name='reduce', ou...]
where the time goes in v3:
time: 67.2 us; the launch traced here: 67 us
  Pallas kernels  65.1 us (97%)
  between operations  1.93 us (3%)
    pallas_call x1, Pallas kernels, reduce_call(): pl.pallas_call(functools.partial(reduce_kernel, ysize), name='reduce', ou...  48.1 us
    pallas_call x1, Pallas kernels, solve_call(): pl.pallas_call(solve_kernel, name='solve', out_shape=(sds(PARAMS, PARAMS)...  17 us

profile of v3, /device:TPU:1, one launch (start us, length us, event | category | flops | bytes accessed | tf_op | source)
XLA Modules:
  0.0 67.0 jit_solution(15748940172155805581)
XLA Ops:
  1.9 48.1 %reduce.1 = (f32[1032,128]{1,0:T(8,128)}, f32[64,256]{1,0:T(8,128)}, f32[8,256]{1,0:T(8,128)}, f32[1,256]{1,0:T(1,128)}) custom-call(s32[1]{0:T(128)S(6)} %copy.11.refs_0_, f32[256,128]{1,0:T(8,128)} %bitcast.10, s32[16,128]{1,0:T(8,128)} %bitcast.13, s32[16,128]{1,0:T(8,128)} %bitcast.14, f32[16,128]{1,0:T(8,128)} %bitcast.15, f32[8,64]{1,0:T(8,128)} %bitcast.11, ...), custom_call_target="tpu_custom_call" | custom-call | tf_op jit(solution)/shard_map/reduce/pallas_call | solution.py:394
  50.0 17.0 %solve.1 = (f32[512,512]{1,0:T(8,128)}, f32[8,64]{1,0:T(8,128)}, f32[2,128]{1,0:T(2,128)}) custom-call(f32[1032,128]{1,0:T(8,128)} %get-tuple-element.10.x_ref, f32[64,256]{1,0:T(8,128)} %get-tuple-element.11.slope_ref, f32[8,256]{1,0:T(8,128)} %get-tuple-element.12.phi_ref, f32[1,256]{1,0:T(1,128)} %get-tuple-element.13.resid_ref, f32[8,64]{1,0:T(8,128)} %bitcast.12, ...), custom_call_target="tpu_custom_call" | custom-call | tf_op jit(solution)/shard_map/solve/pallas_call | solution.py:419

commit v4 on v3

--- a/solution.py
+++ b/solution.py
@@ -26,6 +26,7 @@
 QUARTERS = 4
 ROWS = len(BLOCKS) * NB
 EXTRA = 8
+DAMP_ROW = ROWS + EXTRA - 1
 
 
 def dot(a, b, dims):
@@ -72,7 +73,7 @@
     pix = own(pix_ref)
     slots = pix.shape[1]
     place = col * slots + iota((1, slots), 1)
-    live = ((place < count_ref[0]) & (own(mask_ref) == 1)).astype(F32)
+    live = ((place < count_ref[...]) & (own(mask_ref) == 1)).astype(F32)
 
     img = img_ref[...]
     src = iota((img.shape[0], slots), 0)
@@ -123,10 +124,12 @@
 
 
 def reduce_kernel(ysize, *refs):
-    sum_ref, slope_ref, phi_ref, resid_ref = refs[7:11]
-    own, got0, part, got1, zout, got2, zall, full, e0, e1, e2 = refs[11:22]
-    (s0, r0), (s1, r1), (s2, r2), (s3, r3), (s4, r4), (s5, r5) = zip(refs[22:34:2], refs[23:34:2])
-    (t0, v0), (t1, v1), (t2, v2) = zip(refs[34::2], refs[35::2])
+    args, held, in_sems = refs[:8], refs[13:21], refs[21]
+    sum_ref, slope_ref, phi_ref, resid_ref, theta_out = refs[8:13]
+    refs = refs[22:]
+    own, got0, part, got1, zout, got2, zall, full, e0, e1, e2 = refs[:11]
+    (s0, r0), (s1, r1), (s2, r2), (s3, r3), (s4, r4), (s5, r5) = zip(refs[11:23:2], refs[12:23:2])
+    (t0, v0), (t1, v1), (t2, v2) = zip(refs[23::2], refs[24::2])
     row = lax.axis_index("rows")
     col = lax.axis_index("cols")
     y, z = row // ZN, lax.rem(row, ZN)
@@ -147,11 +150,18 @@
     peers.append([near * 4 + lax.rem(z + d, 4) for d in range(1, 4)])
     zs = [q for group in peers for q in group]
 
+    loads = [pltpu.make_async_copy(a, h, in_sems.at[i]) for i, (a, h) in enumerate(zip(args, held))]
+    for c in loads:
+        c.start()
+
     barrier = pltpu.get_barrier_semaphore()
     for dev in [partner] + [at_plane(p) for p in planes] + [at_z(q) for q in zs]:
         pl.semaphore_signal(barrier, inc=1, device_id=dev, device_id_type=MESH)
 
-    e0[core] = local_terms(*refs[:7], slope_ref, phi_ref, resid_ref, own)
+    for c in loads:
+        c.wait()
+    theta_out[...] = held[5][...]
+    e0[core] = local_terms(*held[:7], slope_ref, phi_ref, resid_ref, own)
 
     pl.semaphore_wait(barrier, 1 + 2 * 15)
 
@@ -227,6 +237,7 @@
     for q in range(1, ZN):
         acc = acc + e2[q]
     sum_ref[ROWS:ROWS + EXTRA, :] = acc
+    sum_ref[DAMP_ROW:DAMP_ROW + 1, :] = jnp.broadcast_to(held[7][...], (1, NB))
     for k in near_first:
         for p in planes:
             got = full.at[tile_of(core, k, p)]
@@ -310,11 +321,15 @@
     return ws
 
 
-def solve_kernel(x_ref, slope_ref, phi_ref, resid_ref, theta_ref, damp_ref,
-                 r_ref, theta_out, pred_ref, a_ref, w_ref, g_ref, y_ref):
+def solve_kernel(x_ref, slope_ref, phi_ref, resid_ref, theta_ref,
+                 r_out, theta_out, pred_ref, r_ref, a_ref, w_ref, g_ref, y_ref, sems):
+    def put(b):
+        rows = pl.ds(b * NB, NB)
+        return pltpu.make_async_copy(r_ref.at[rows], r_out.at[rows], sems.at[b])
+
     inv_total = 1.0 / x_ref[ROWS + 6:ROWS + 7, :]
     same = iota((NB, NB), 0) == iota((NB, NB), 1)
-    eye = same.astype(F32) * damp_ref[0]
+    eye = same.astype(F32) * x_ref[DAMP_ROW:DAMP_ROW + 1, :]
     upper = iota((NB, NB), 0) <= iota((NB, NB), 1)
     for k, (i, j) in enumerate(BLOCKS):
         v = x_ref[k * NB:(k + 1) * NB, :] * inv_total
@@ -333,30 +348,23 @@
             r_ref[i * NB:(i + 1) * NB, j * NB:(j + 1) * NB] = jnp.zeros((NB, NB), F32)
         g_ref[i] = x_ref[ROWS + i:ROWS + i + 1, :] * inv_total
 
-    def body(b, carry):
-        at = pl.multiple_of(b * NB, NB)
-        ws = factor_block([a_ref[pl.ds(at + 8 * s, 8), pl.ds(at, NB)] for s in range(16)])
-        for s in range(16):
-            w_ref[b, 8 * s:8 * s + 8, :] = ws[s]
-        for k in range(4):
-            @pl.when(b == k)
-            def _():
-                lo, hi = k * NB, (k + 1) * NB
-                w = w_ref[k]
-                panel = dot(w, a_ref[lo:hi, lo:], NN)
-                r_ref[lo:hi, lo:hi] = jnp.where(upper, panel[:, :NB], 0.0)
-                y = jnp.sum(w * g_ref[k], axis=1, keepdims=True)
-                y_ref[k] = y
-                if k < 3:
-                    r_ref[lo:hi, hi:] = panel[:, NB:]
-                for c in range(k + 1, 4):
-                    off = c * NB - lo
-                    piece = panel[:, off:off + NB]
-                    a_ref[c * NB:(c + 1) * NB, c * NB:] -= dot(piece, panel[:, off:], TN)
-                    g_ref[c] = g_ref[c] - jnp.sum(piece * y, axis=0, keepdims=True)
-        return carry
-
-    lax.fori_loop(0, 4, body, 0)
+    for b in range(4):
+        lo, hi = b * NB, (b + 1) * NB
+        ws = factor_block([a_ref[lo + 8 * s:lo + 8 * s + 8, lo:hi] for s in range(16)])
+        w = jnp.concatenate(ws, axis=0)
+        w_ref[b] = w
+        y = jnp.sum(w * g_ref[b], axis=1, keepdims=True)
+        y_ref[b] = y
+        panel = dot(w, a_ref[lo:hi, lo:], NN)
+        for c in range(b + 1, 4):
+            off = c * NB - lo
+            piece = panel[:, off:off + NB]
+            a_ref[c * NB:(c + 1) * NB, c * NB:] -= dot(piece, panel[:, off:], TN)
+            g_ref[c] = g_ref[c] - jnp.sum(piece * y, axis=0, keepdims=True)
+        r_ref[lo:hi, lo:hi] = jnp.where(upper, panel[:, :NB], 0.0)
+        if b < 3:
+            r_ref[lo:hi, hi:] = panel[:, NB:]
+        put(b).start()
     xs = [None] * 4
     for b in reversed(range(4)):
         z = y_ref[b]
@@ -375,11 +383,12 @@
     moved = dot(step, phi_ref[...], TN)
     pred = resid_ref[...] + jnp.sum(slope_ref[...] * moved, axis=0, keepdims=True)
     pred_ref[...] = jnp.concatenate([pred[:, :NB], pred[:, NB:]], axis=0)
+    for b in range(4):
+        put(b).wait()
 
 
 THETA_T = True
 VM = pl.BlockSpec(memory_space=pltpu.VMEM)
-SM = pl.BlockSpec(memory_space=pltpu.SMEM)
 
 
 def sds(*shape):
@@ -394,10 +403,11 @@
     return pl.pallas_call(
         functools.partial(reduce_kernel, ysize),
         name="reduce",
-        out_shape=(sds(ROWS + EXTRA, NB), sds(chans, slots), sds(basis, slots), sds(1, slots)),
-        in_specs=[SM] + [VM] * 6,
-        out_specs=(VM,) * 4,
-        scratch_shapes=[
+        out_shape=tuple(pltpu.VMEM(d, F32) for d in ((ROWS + EXTRA, NB), (chans, slots), (basis, slots), (1, slots), (basis, chans))),
+        in_specs=[pl.BlockSpec(memory_space=pl.ANY)] * 8,
+        out_specs=(VM,) * 5,
+        scratch_shapes=[pltpu.VMEM(a.shape, a.dtype) for a in args] + [
+            dma((8,)),
             pltpu.VMEM((ROWS, NB), F32),
             pltpu.VMEM((QUARTERS, NB, NB), F32),
             pltpu.VMEM((QUARTERS, NB, NB), F32),
@@ -414,32 +424,34 @@
     )(*args)
 
 
-def solve_call(summed, slope, phi, resid, theta, damping):
+def solve_call(summed, slope, phi, resid, theta):
     slots = resid.shape[1]
     return pl.pallas_call(
         solve_kernel,
         name="solve",
         out_shape=(sds(PARAMS, PARAMS), sds(*theta.shape), sds(slots // NB, NB)),
-        in_specs=[VM] * 5 + [SM],
-        out_specs=(VM,) * 3,
+        in_specs=[VM] * 5,
+        out_specs=(pl.BlockSpec(memory_space=pl.ANY), VM, VM),
         scratch_shapes=[
+            pltpu.VMEM((PARAMS, PARAMS), F32),
             pltpu.VMEM((PARAMS, PARAMS), F32),
             pltpu.VMEM((4, NB, NB), F32),
             pltpu.VMEM((4, 1, NB), F32),
             pltpu.VMEM((4, NB, 1), F32),
+            pltpu.SemaphoreType.DMA((4,)),
         ],
-    )(summed, slope, phi, resid, theta, damping)
+        compiler_params=pltpu.CompilerParams(vmem_limit_bytes=24 << 20),
+    )(summed, slope, phi, resid, theta)
 
 
 def on_device(images, gauge_pixel, row_mask, gauge_counts, targets, theta, amplitude, damping):
     def lanes(v):
         return v.reshape(-1, NB)
 
-    summed, slope, phi, resid = reduce_call(
-        4, gauge_counts, images.reshape(-1, NB), lanes(gauge_pixel), lanes(row_mask),
-        lanes(targets), theta.T, amplitude.reshape(1, -1))
-    r, new_theta, pred = solve_call(
-        summed, slope, phi, resid, theta.T, damping.reshape(1))
+    terms = reduce_call(
+        4, gauge_counts.reshape(1, 1), images.reshape(-1, NB), lanes(gauge_pixel), lanes(row_mask),
+        lanes(targets), theta.T, amplitude.reshape(1, -1), damping.reshape(1, 1))
+    r, new_theta, pred = solve_call(*terms)
     return r, new_theta.T, pred.reshape(-1)
 
 

time: 67.2 us -> 64.3 us (0.957)
  Pallas kernels: 65.1 us -> 62 us
    pallas_call x1, Pallas kernels: 17 us -> 15.3 us  [solve_call(): pl.pallas_call(solve_kernel, name='solve', out_shape=(sds(PARAMS, PARAMS)...]
    pallas_call x1, Pallas kernels: 48.1 us -> 46.7 us  [reduce_call(): pl.pallas_call(functools.partial(reduce_kernel, ysize), name='reduce', ou...]
where the time goes in v4:
time: 64.3 us; the launch traced here: 64.1 us
  Pallas kernels  62 us (96%)
  between operations  2.09 us (3%)
    pallas_call x1, Pallas kernels, reduce_call(): pl.pallas_call(functools.partial(reduce_kernel, ysize), name='reduce', ou...  46.7 us
    pallas_call x1, Pallas kernels, solve_call(): pl.pallas_call(solve_kernel, name='solve', out_shape=(sds(PARAMS, PARAMS)...  15.3 us

profile of v4, /device:TPU:1, one launch (start us, length us, event | category | flops | bytes accessed | tf_op | source)
XLA Modules:
  0.0 64.1 jit_solution(13739855006611948891)
XLA Ops:
  1.9 46.7 %reduce.1 = (f32[1032,128]{1,0:T(8,128)S(1)}, f32[64,256]{1,0:T(8,128)S(1)}, f32[8,256]{1,0:T(8,128)S(1)}, f32[1,256]{1,0:T(1,128)S(1)}, f32[8,64]{1,0:T(8,128)S(1)}) custom-call(s32[1,1]{1,0:T(1,128)} %bitcast.10.refs_0_, f32[256,128]{1,0:T(8,128)} %bitcast.12, s32[16,128]{1,0:T(8,128)} %bitcast.13, s32[16,128]{1,0:T(8,128)} %bitcast.14, ...), custom_call_target="tpu_custom_call" | custom-call | tf_op jit(solution)/shard_map/reduce/pallas_call | solution.py:403
  48.6 15.3 %solve.1 = (f32[512,512]{1,0:T(8,128)}, f32[8,64]{1,0:T(8,128)}, f32[2,128]{1,0:T(2,128)}) custom-call(f32[1032,128]{1,0:T(8,128)S(1)} %get-tuple-element.11.x_ref, f32[64,256]{1,0:T(8,128)S(1)} %get-tuple-element.12.slope_ref, f32[8,256]{1,0:T(8,128)S(1)} %get-tuple-element.13.phi_ref, f32[1,256]{1,0:T(1,128)S(1)} %get-tuple-element.14.resid_ref, ...), custom_call_target="tpu_custom_call" | custom-call | tf_op jit(solution)/shard_map/solve/pallas_call | solution.py:429

commit v5 on v4

--- a/solution.py
+++ b/solution.py
@@ -31,6 +31,24 @@
 
 def dot(a, b, dims):
     return lax.dot_general(a, b, dims, precision=HI, preferred_element_type=F32)
+
+
+def parts(v):
+    def head(x):
+        return x.astype(jnp.bfloat16).astype(F32)
+
+    h = head(v)
+    m = head(v - h)
+    return h, m, v - h - m
+
+
+def dot6(a, b, dims):
+    da, db = dims[0][0][0], dims[0][1][0]
+    ah, am, al = (t.astype(jnp.bfloat16) for t in parts(a))
+    bh, bm, bl = (t.astype(jnp.bfloat16) for t in parts(b))
+    left = jnp.concatenate([al, am, ah, am, ah, ah], axis=da)
+    right = jnp.concatenate([bh, bm, bl, bh, bm, bh], axis=db)
+    return lax.dot_general(left, right, dims, preferred_element_type=F32)
 
 
 def norm_of(order, width):
@@ -145,7 +163,10 @@
         return {"rows": y * ZN + q, "cols": col}
 
     partner = {"rows": row, "cols": x * 2 + 1 - core}
-    planes = [lax.rem(me + d, PLANE) for d in range(1, PLANE)]
+    shifts = [(i, j) for i in range(PLANE // ysize) for j in range(ysize)][1:]
+    shifts.sort(key=lambda d: -min(d[0], PLANE // ysize - d[0]) - min(d[1], ysize - d[1]))
+    planes = [
+        lax.rem(x + i, PLANE // ysize) * ysize + lax.rem(y + j, ysize) for i, j in shifts]
     peers = [[k * 4 + d for d in range(4)] for k in far_first[:3]]
     peers.append([near * 4 + lax.rem(z + d, 4) for d in range(1, 4)])
     zs = [q for group in peers for q in group]
@@ -355,11 +376,11 @@
         w_ref[b] = w
         y = jnp.sum(w * g_ref[b], axis=1, keepdims=True)
         y_ref[b] = y
-        panel = dot(w, a_ref[lo:hi, lo:], NN)
+        panel = dot6(w, a_ref[lo:hi, lo:], NN)
         for c in range(b + 1, 4):
             off = c * NB - lo
             piece = panel[:, off:off + NB]
-            a_ref[c * NB:(c + 1) * NB, c * NB:] -= dot(piece, panel[:, off:], TN)
+            a_ref[c * NB:(c + 1) * NB, c * NB:] -= dot6(piece, panel[:, off:], TN)
             g_ref[c] = g_ref[c] - jnp.sum(piece * y, axis=0, keepdims=True)
         r_ref[lo:hi, lo:hi] = jnp.where(upper, panel[:, :NB], 0.0)
         if b < 3:
@@ -377,8 +398,11 @@
     step_row = -jnp.concatenate(xs, axis=1)
     basis, chans = theta_ref.shape
     own = (iota((basis, PARAMS), 1) & 7) == iota((basis, PARAMS), 0)
-    pick = ((iota((PARAMS, chans), 0) >> 3) == iota((PARAMS, chans), 1)).astype(F32)
-    step = dot(jnp.where(own, step_row, 0.0), pick, NN)
+    pick = ((iota((PARAMS, chans), 0) >> 3) == iota((PARAMS, chans), 1)).astype(jnp.bfloat16)
+    rows = [jnp.where(own, t, 0.0).astype(jnp.bfloat16) for t in parts(step_row)]
+    three = lax.dot_general(
+        jnp.concatenate(rows[::-1], axis=0), pick, NN, preferred_element_type=F32)
+    step = three[:basis] + three[basis:2 * basis] + three[2 * basis:]
     theta_out[...] = theta_ref[...] + step
     moved = dot(step, phi_ref[...], TN)
     pred = resid_ref[...] + jnp.sum(slope_ref[...] * moved, axis=0, keepdims=True)

time: 64.3 us -> 62.8 us (0.977)
  Pallas kernels: 62 us -> 60.5 us
    pallas_call x1, Pallas kernels: 15.3 us -> 14.2 us  [solve_call(): pl.pallas_call(solve_kernel, name='solve', out_shape=(sds(PARAMS, PARAMS)...]
where the time goes in v5:
time: 62.8 us; the launch traced here: 62.6 us
  Pallas kernels  60.5 us (96%)
  between operations  2.09 us (3%)
    pallas_call x1, Pallas kernels, reduce_call(): pl.pallas_call(functools.partial(reduce_kernel, ysize), name='reduce', ou...  46.4 us
    pallas_call x1, Pallas kernels, solve_call(): pl.pallas_call(solve_kernel, name='solve', out_shape=(sds(PARAMS, PARAMS)...  14.2 us

profile of v5, /device:TPU:1, one launch (start us, length us, event | category | flops | bytes accessed | tf_op | source)
XLA Modules:
  0.0 62.6 jit_solution(6737057857616038766)
XLA Ops:
  1.9 46.4 %reduce.1 = (f32[1032,128]{1,0:T(8,128)S(1)}, f32[64,256]{1,0:T(8,128)S(1)}, f32[8,256]{1,0:T(8,128)S(1)}, f32[1,256]{1,0:T(1,128)S(1)}, f32[8,64]{1,0:T(8,128)S(1)}) custom-call(s32[1,1]{1,0:T(1,128)} %bitcast.10.refs_0_, f32[256,128]{1,0:T(8,128)} %bitcast.12, s32[16,128]{1,0:T(8,128)} %bitcast.13, s32[16,128]{1,0:T(8,128)} %bitcast.14, ...), custom_call_target="tpu_custom_call" | custom-call | tf_op jit(solution)/shard_map/reduce/pallas_call | solution.py:427
  48.3 14.2 %solve.1 = (f32[512,512]{1,0:T(8,128)}, f32[8,64]{1,0:T(8,128)}, f32[2,128]{1,0:T(2,128)}) custom-call(f32[1032,128]{1,0:T(8,128)S(1)} %get-tuple-element.11.x_ref, f32[64,256]{1,0:T(8,128)S(1)} %get-tuple-element.12.slope_ref, f32[8,256]{1,0:T(8,128)S(1)} %get-tuple-element.13.phi_ref, f32[1,256]{1,0:T(1,128)S(1)} %get-tuple-element.14.resid_ref, ...), custom_call_target="tpu_custom_call" | custom-call | tf_op jit(solution)/shard_map/solve/pallas_call | solution.py:453

commit v6 on v5

--- a/solution.py
+++ b/solution.py
@@ -244,6 +244,7 @@
     zall[z] = tot
     for q in zs:
         start(zall.at[z], zall.at[z], s3.at[q], r3.at[z], at_z(q))
+    early = len(sends)
     near_first = list(reversed(far_first))
     for k, group in zip(near_first, reversed(peers)):
         for q in group:
@@ -257,6 +258,8 @@
     acc = e2[0]
     for q in range(1, ZN):
         acc = acc + e2[q]
+    for c in sends[:early]:
+        c.wait_send()
     sum_ref[ROWS:ROWS + EXTRA, :] = acc
     sum_ref[DAMP_ROW:DAMP_ROW + 1, :] = jnp.broadcast_to(held[7][...], (1, NB))
     for k in near_first:
@@ -265,12 +268,13 @@
             copy(got, got, s4.at[k, p], r4.at[k, p], at_plane(p)).wait_recv()
         mine = full.at[block(core, k)]
         start(mine, mine, s5.at[k], r5.at[k], partner)
+        sum_ref[block(core, k), :] = mine[...]
+    for c in sends[early:]:
+        c.wait_send()
     for k in near_first:
         got = full.at[block(1 - core, k)]
         copy(got, got, s5.at[k], r5.at[k], partner).wait_recv()
-    for c in sends:
-        c.wait_send()
-    sum_ref[0:ROWS, :] = full[...]
+        sum_ref[block(1 - core, k), :] = got[...]
 
 
 def lane(v, c):

time: 62.8 us -> 62.4 us (level)
  no operation moved by 1% of the time
where the time goes in v6:
time: 62.4 us; the launch traced here: 62.3 us
  Pallas kernels  60.2 us (96%)
  between operations  2.09 us (3%)
    pallas_call x1, Pallas kernels, reduce_call(): pl.pallas_call(functools.partial(reduce_kernel, ysize), name='reduce', ou...  46 us
    pallas_call x1, Pallas kernels, solve_call(): pl.pallas_call(solve_kernel, name='solve', out_shape=(sds(PARAMS, PARAMS)...  14.2 us

profile of v6, /device:TPU:1, one launch (start us, length us, event | category | flops | bytes accessed | tf_op | source)
XLA Modules:
  0.0 62.3 jit_solution(4093438412702315284)
XLA Ops:
  1.9 46.0 %reduce.1 = (f32[1032,128]{1,0:T(8,128)S(1)}, f32[64,256]{1,0:T(8,128)S(1)}, f32[8,256]{1,0:T(8,128)S(1)}, f32[1,256]{1,0:T(1,128)S(1)}, f32[8,64]{1,0:T(8,128)S(1)}) custom-call(s32[1,1]{1,0:T(1,128)} %bitcast.10.refs_0_, f32[256,128]{1,0:T(8,128)} %bitcast.12, s32[16,128]{1,0:T(8,128)} %bitcast.13, s32[16,128]{1,0:T(8,128)} %bitcast.14, ...), custom_call_target="tpu_custom_call" | custom-call | tf_op jit(solution)/shard_map/reduce/pallas_call | solution.py:431
  48.0 14.2 %solve.1 = (f32[512,512]{1,0:T(8,128)}, f32[8,64]{1,0:T(8,128)}, f32[2,128]{1,0:T(2,128)}) custom-call(f32[1032,128]{1,0:T(8,128)S(1)} %get-tuple-element.11.x_ref, f32[64,256]{1,0:T(8,128)S(1)} %get-tuple-element.12.slope_ref, f32[8,256]{1,0:T(8,128)S(1)} %get-tuple-element.13.phi_ref, f32[1,256]{1,0:T(1,128)S(1)} %get-tuple-element.14.resid_ref, ...), custom_call_target="tpu_custom_call" | custom-call | tf_op jit(solution)/shard_map/solve/pallas_call | solution.py:457
